TPU v7x, 32 devices: a whole 2x2x4 slice. The times are simulated.
32 devices in a mesh: seq: 4 (over x, core), head: 8 (over z, y).
Axes of the slice: x: 2, y: 2, z: 4, core: 2. Of those that a mesh axis runs over, the one named last changes fastest.
Arguments:
- inner_input: bfloat16 [2048, 16384], P('seq', 'head'), may hold values from -6 to 6
- gate_input: bfloat16 [2048, 16384], P('seq', 'head'), may hold values from -48 to 48
- bc_input: bfloat16 [2048, 4096], P('seq'), may hold values from -6 to 6
- dt_input: float32 [256, 2048], P('head', 'seq'), may hold values from -11.5 to 0
- log_rate: float32 [256], P('head'), may hold values from -1.2 to 0
- skip_weight: float32 [256], P('head'), may hold values from 0.5 to 1.5
- conv_weight_x: float32 [4, 16384], P(None, 'head'), may hold values from -3 to 3
- conv_bias_x: float32 [16384], P('head'), may hold values from -3 to 3
- conv_weight_bc: float32 [4, 4096], replicated, may hold values from -3 to 3
- conv_bias_bc: float32 [4096], replicated, may hold values from -3 to 3
- conv_tail_x: bfloat16 [3, 16384], P(None, 'head'), may hold values from -6 to 6
- conv_tail_bc: bfloat16 [3, 4096], replicated, may hold values from -6 to 6
- init_state: float32 [256, 64, 256], P('head'), may hold values from -0.6 to 0.6
- norm_gain: float32 [16384], P('head'), may hold values from 0.5 to 1.5
- out_weight: bfloat16 [16384, 8192], P('head', 'seq'), may hold values from -0.046875 to 0.046875
Outputs:
- layer_out: bfloat16 [2048, 8192], P(('seq', 'head'))
- boundary_states: float32 [4, 256, 64, 256], P('seq', 'head')
All inputs are finite; a program needn't handle non-finite values.
Results may differ from a plain program's by a relative error of at most 0.015.
Values may be sent and summed in bfloat16 or wider, within the bound.
A program may use at most 192 MiB of HBM per device.

v0:
```python
import jax
import jax.numpy as jnp
from jax import lax
from jax.sharding import PartitionSpec as P

MIXER_HEADS = 256
HEADDIM = 64
STATE = 256
GROUPS = 8
KERNEL = 4
SPAN = 128
DINNER = 16384


highest = lax.Precision.HIGHEST
norm_eps = 1e-05


def from_behind(x, axis, by):
    count = lax.axis_size(axis)
    pairs = [(i, i + by) for i in range(count) if 0 <= i + by < count]
    return lax.ppermute(x, axis, pairs)


def carried_in(x, axis, join, neutral):
    place = lax.axis_index(axis)
    gathered = jax.tree.map(
        lambda a, kind: lax.all_gather(a.astype(kind), axis), x, (jnp.bfloat16, jnp.bfloat16)
    )
    state = jax.tree.map(lambda a, e: jnp.zeros_like(a) + jnp.asarray(e, a.dtype), x, neutral)

    def one(lap, state):
        return join(
            state,
            jax.tree.map(
                lambda a, own: lax.dynamic_index_in_dim(a, lap, 0, False).astype(own.dtype),
                gathered,
                x,
            ),
        )

    return lax.fori_loop(0, place, one, state)


def causal_conv(values, previous, kernel_weight, kernel_bias):
    extended = jnp.concatenate([previous, values], axis=0)
    length = values.shape[0]
    running = jnp.zeros_like(values) + kernel_bias[None, :]
    for offset in range(KERNEL):
        running = running + kernel_weight[offset][None, :] * extended[offset : offset + length]
    return running


def ssd_block(span_x, span_b, span_c, span_step, span_log, state):
    cumul = jnp.cumsum(span_log, axis=1)
    length = span_x.shape[0]
    causal = (jnp.arange(length)[:, None] >= jnp.arange(length)[None, :])[None]
    spread = jnp.where(causal, cumul[:, :, None] - cumul[:, None, :], 0.0)
    decays = jnp.where(causal, jnp.exp(spread), 0.0)
    scores = jnp.einsum("thn,shn->hts", span_c, span_b, precision=highest)
    mixer = scores * decays * span_step[:, None, :]
    output = jnp.einsum("hts,shp->thp", mixer, span_x, precision=highest)
    carried = jnp.einsum("thn,hpn->thp", span_c, state, precision=highest)
    output = output + jnp.exp(cumul).T[:, :, None] * carried
    weights = jnp.exp(cumul[:, -1:] - cumul) * span_step
    written = jnp.einsum("hs,shp,shn->hpn", weights, span_x, span_b, precision=highest)
    new_state = jnp.exp(cumul[:, -1])[:, None, None] * state + written
    return (output, new_state)


def body(
    inner_input,
    gate_input,
    bc_input,
    dt_input,
    log_rate,
    skip_weight,
    conv_weight_x,
    conv_bias_x,
    conv_weight_bc,
    conv_bias_bc,
    conv_tail_x,
    conv_tail_bc,
    init_state,
    norm_gain,
    out_weight,
):
    seq_index = lax.axis_index("seq")
    head_index = lax.axis_index("head")
    row_count = inner_input.shape[0]
    channels = inner_input.shape[1]
    heads_here = dt_input.shape[0]
    per_group = MIXER_HEADS // GROUPS
    heads_shared = min(heads_here, per_group)
    groups_here = heads_here // heads_shared
    group_first = head_index * heads_here // per_group
    width_bc = groups_here * STATE

    def own_columns(table, table_dim):
        part_b = lax.dynamic_slice_in_dim(table, group_first * STATE, width_bc, table_dim)
        part_c = lax.dynamic_slice_in_dim(
            table, GROUPS * STATE + group_first * STATE, width_bc, table_dim
        )
        return jnp.concatenate([part_b, part_c], axis=table_dim)

    own_bc = own_columns(bc_input, 1)
    tail_rows = row_count - KERNEL + 1
    arrived = from_behind((inner_input[tail_rows:], own_bc[tail_rows:]), "seq", 1)
    at_first = seq_index == 0
    previous_x = jnp.where(at_first, conv_tail_x, arrived[0])
    previous_bc = jnp.where(at_first, own_columns(conv_tail_bc, 1), arrived[1])
    conv_x = jax.nn.silu(
        causal_conv(
            inner_input.astype(jnp.float32),
            previous_x.astype(jnp.float32),
            conv_weight_x,
            conv_bias_x,
        )
    ).astype(jnp.bfloat16)
    conv_bc = jax.nn.silu(
        causal_conv(
            own_bc.astype(jnp.float32),
            previous_bc.astype(jnp.float32),
            own_columns(conv_weight_bc, 1),
            own_columns(conv_bias_bc, 0),
        )
    ).astype(jnp.bfloat16)
    stride_length = jax.nn.softplus(dt_input)
    decay_log = -jnp.exp(log_rate)[:, None] * stride_length
    spans_here = row_count // SPAN
    all_x = conv_x.astype(jnp.float32).reshape(row_count, heads_here, HEADDIM)
    bc_float = conv_bc.astype(jnp.float32)
    all_b = jnp.repeat(
        bc_float[:, :width_bc].reshape(row_count, groups_here, STATE), heads_shared, axis=1
    )
    all_c = jnp.repeat(
        bc_float[:, width_bc:].reshape(row_count, groups_here, STATE), heads_shared, axis=1
    )

    def span_step_body(state, span_index):
        first_row = span_index * SPAN
        span_x = lax.dynamic_slice_in_dim(all_x, first_row, SPAN, 0)
        span_b = lax.dynamic_slice_in_dim(all_b, first_row, SPAN, 0)
        span_c = lax.dynamic_slice_in_dim(all_c, first_row, SPAN, 0)
        span_step = lax.dynamic_slice_in_dim(stride_length, first_row, SPAN, 1)
        span_log = lax.dynamic_slice_in_dim(decay_log, first_row, SPAN, 1)
        output, new_state = ssd_block(span_x, span_b, span_c, span_step, span_log, state)
        return (new_state, output)

    empty_state = jnp.zeros((heads_here, HEADDIM, STATE), jnp.float32)
    local_state, local_out = lax.scan(
        span_step_body, empty_state, jnp.arange(spans_here, dtype=jnp.int32)
    )
    local_out = local_out.reshape(row_count, heads_here, HEADDIM)
    cumul = jnp.cumsum(decay_log, axis=1)
    total_log = cumul[:, -1]

    def combine(earlier, later):
        return (earlier[0] + later[0], jnp.exp(later[0])[:, None, None] * earlier[1] + later[1])

    identity = (jnp.zeros((heads_here,), jnp.float32), empty_state)
    prior_log, prior_state = carried_in((total_log, local_state), "seq", combine, identity)
    incoming = jnp.exp(prior_log)[:, None, None] * init_state + prior_state
    incoming_term = jnp.einsum("thn,hpn->thp", all_c, incoming, precision=highest)
    outputs = (
        local_out
        + jnp.exp(cumul).T[:, :, None] * incoming_term
        + skip_weight[None, :, None] * all_x
    )
    boundary = (jnp.exp(total_log)[:, None, None] * incoming + local_state)[None]
    mixed = outputs.reshape(row_count, channels) * jax.nn.silu(gate_input.astype(jnp.float32))
    group_width = DINNER // GROUPS
    piece_width = min(channels, group_width)
    pieces_here = channels // piece_width
    pieces = mixed.reshape(row_count, pieces_here, piece_width)
    squares = jnp.sum(pieces * pieces, axis=2).T
    own_group = (head_index * pieces_here + jnp.arange(pieces_here)) * piece_width // group_width
    membership = (own_group[:, None] == jnp.arange(GROUPS)[None, :]).astype(jnp.float32)
    contribution = jnp.dot(membership.T, squares, precision=highest)
    group_totals = lax.psum(contribution, "head")
    group_sums = jnp.dot(membership, group_totals, precision=highest)
    inverse_rms = lax.rsqrt(group_sums / group_width + norm_eps).T
    normed = (
        (pieces * inverse_rms[:, :, None]).reshape(row_count, channels) * norm_gain[None, :]
    ).astype(jnp.bfloat16)
    terms = jnp.dot(
        normed,
        lax.all_gather(out_weight, "seq", axis=1, tiled=True),
        preferred_element_type=jnp.float32,
    )
    layer_out = lax.psum_scatter(
        terms.astype(jnp.bfloat16), "head", scatter_dimension=0, tiled=True
    )
    return (layer_out, boundary)


def solution(mesh):
    in_specs = (
        P("seq", "head"),
        P("seq", "head"),
        P("seq", None),
        P("head", "seq"),
        P("head"),
        P("head"),
        P(None, "head"),
        P("head"),
        P(),
        P(),
        P(None, "head"),
        P(),
        P("head", None, None),
        P("head"),
        P("head", "seq"),
    )
    out_specs = (P(("seq", "head"), None), P("seq", "head", None, None))
    return jax.shard_map(body, mesh=mesh, in_specs=in_specs, out_specs=out_specs, check_vma=False)
```

profile of v0, /device:TPU:0, one launch (start us, length us, event | category | flops | bytes accessed | tf_op | source)
XLA Modules:
  0.0 697.1 jit_solution(13256864626759303394)
XLA Ops:
  7.2 1.2 constant_dynamic-slice_fusion.4
  8.5 2.4 collective-permute-start.1
  10.9 0.8 slice.68
  11.6 4.5 collective-permute-start
  16.3 0.7 constant_dynamic-slice_fusion.6
  17.0 0.7 constant_dynamic-slice_fusion.8
  17.7 0.8 fusion.99
  18.5 0.9 fusion.98
  19.4 0.7 exponential_negate_fusion
  20.1 0.9 compare_select_fusion
  21.0 2.5 convert_element_type.65
  23.5 0.7 fusion.84
  24.3 1.5 copy-done
  25.9 4.0 fusion.73
  29.9 5.4 copy.32
  35.2 7.6 %reshape.131 = f32[512,32,256]{2,0,1:T(8,128)} broadcast(f32[512,256]{1,0:T(8,128)S(1)} %get-tuple-element.156), dimensions={0,2} | broadcast | bytes 17301504 | tf_op jit(solution)/shard_map/reshape | solution.py:133
  42.9 7.6 %reshape.132 = f32[512,32,256]{2,0,1:T(8,128)} broadcast(f32[512,256]{1,0:T(8,128)S(1)} %get-tuple-element.155), dimensions={0,2} | broadcast | bytes 17301504 | tf_op jit(solution)/shard_map/reshape | solution.py:136
  50.5 222.8 %while.26 = (s32[]{:T(128)}, f32[32,64,256]{2,1,0:T(8,128)S(1)}, f32[4,128,32,64]{1,0,3,2:T(4,128)}, s32[4]{0:T(128)S(1)}, f32[32,512]{1,0:T(8,128)S(1)}, /*inde...) while((s32[]{:T(128)}, f32[32,64,256]{2,1,0:T(8,128)S(1)}, ...), condition=%wide.region_2.3_spmd.clone, body=%wide.region_0.2_spmd.clone.sunk | while | flops 3629928448 | bytes 34868704 | solution.py:151
  50.5 0.6 dynamic_slice.123
  51.7 0.3 reduce_window_sum.33
  52.3 7.9 %fusion.122 = f32[32,128,128]{2,1,0:T(8,128)S(1)} fusion(f32[512,32,256]{2,0,1:T(8,128)} %get-tuple-element.312, s32[]{:T(128)S(6)} %select_n.102, f32[512,32,256]{2,0,1:T(8,128)} %get-tuple-element.311), kind=kOutput, calls=%fused_computation.6.clone.1 | convolution fusion | flops 1610612736 | bytes 10486784 | tf_op jit(solution)/shard_map/while/body/eval_jaxpr/thn,shn->hts/dot_general | solution.py:60
  60.2 6.5 fusion.123
  66.7 7.3 %fusion.124 = f32[128,32,64]{0,2,1:T(8,128)S(1)} fusion(f32[128,32,64]{0,2,1:T(8,128)} %fusion.123, f32[32,64,256]{2,1,0:T(8,128)S(1)} %get-tuple-element.291, f32[512,32,256]{2,0,1:T(8,128)} %get-tuple-element.312, s32[]{:T(128)S(6)} %select_n.102, pred[]{:T(512)S(6)} %compare.7, f32[128,32]{0,1:T(8,128)S(1)} %get-tuple-element.275), kind=kOutput, calls=%fused_computation.23.clone.1 | convolution fusion | flops 806354944 | bytes 8404997 | tf_op jit(solution)/shard_map/while/body/eval_jaxpr/thn,hpn->thp/dot_general | solution.py:63
  74.0 26.4 %dynamic_update_slice.6 = f32[4,128,32,64]{1,0,3,2:T(4,128)} dynamic-update-slice(f32[4,128,32,64]{1,0,3,2:T(4,128)} %get-tuple-element.292, f32[1,128,32,64]{1,0,3,2:T(1,128)S(1)} %bitcast.82, s32[]{:T(128)} %get-tuple-element.290, s32[]{:T(128)} %constant.87.clone.1..sunk.1, s32[]{:T(128)} %constant.87.clone.1..sunk.1, s32[]{:T(128)} %constant.87.clone.1..sunk.1) | dynamic-update-slice | bytes 2097156 | tf_op jit(solution)/shard_map/while/body/jit(dynamic_update_index_in_dim)/dynamic_update_slice | solution.py:151
  100.4 5.7 multiply_add_fusion.4
  106.1 0.6 dynamic_slice.123
  107.4 0.3 reduce_window_sum.33
  107.9 7.9 %fusion.122 = f32[32,128,128]{2,1,0:T(8,128)S(1)} fusion(f32[512,32,256]{2,0,1:T(8,128)} %get-tuple-element.312, s32[]{:T(128)S(6)} %select_n.102, f32[512,32,256]{2,0,1:T(8,128)} %get-tuple-element.311), kind=kOutput, calls=%fused_computation.6.clone.1 | convolution fusion | flops 1610612736 | bytes 10486784 | tf_op jit(solution)/shard_map/while/body/eval_jaxpr/thn,shn->hts/dot_general | solution.py:60
  115.8 6.5 fusion.123
  122.3 7.3 %fusion.124 = f32[128,32,64]{0,2,1:T(8,128)S(1)} fusion(f32[128,32,64]{0,2,1:T(8,128)} %fusion.123, f32[32,64,256]{2,1,0:T(8,128)S(1)} %get-tuple-element.291, f32[512,32,256]{2,0,1:T(8,128)} %get-tuple-element.312, s32[]{:T(128)S(6)} %select_n.102, pred[]{:T(512)S(6)} %compare.7, f32[128,32]{0,1:T(8,128)S(1)} %get-tuple-element.275), kind=kOutput, calls=%fused_computation.23.clone.1 | convolution fusion | flops 806354944 | bytes 8404997 | tf_op jit(solution)/shard_map/while/body/eval_jaxpr/thn,hpn->thp/dot_general | solution.py:63
  129.6 26.4 %dynamic_update_slice.6 = f32[4,128,32,64]{1,0,3,2:T(4,128)} dynamic-update-slice(f32[4,128,32,64]{1,0,3,2:T(4,128)} %get-tuple-element.292, f32[1,128,32,64]{1,0,3,2:T(1,128)S(1)} %bitcast.82, s32[]{:T(128)} %get-tuple-element.290, s32[]{:T(128)} %constant.87.clone.1..sunk.1, s32[]{:T(128)} %constant.87.clone.1..sunk.1, s32[]{:T(128)} %constant.87.clone.1..sunk.1) | dynamic-update-slice | bytes 2097156 | tf_op jit(solution)/shard_map/while/body/jit(dynamic_update_index_in_dim)/dynamic_update_slice | solution.py:151
  156.0 5.7 multiply_add_fusion.4
  161.7 0.6 dynamic_slice.123
  163.0 0.3 reduce_window_sum.33
  163.5 7.9 %fusion.122 = f32[32,128,128]{2,1,0:T(8,128)S(1)} fusion(f32[512,32,256]{2,0,1:T(8,128)} %get-tuple-element.312, s32[]{:T(128)S(6)} %select_n.102, f32[512,32,256]{2,0,1:T(8,128)} %get-tuple-element.311), kind=kOutput, calls=%fused_computation.6.clone.1 | convolution fusion | flops 1610612736 | bytes 10486784 | tf_op jit(solution)/shard_map/while/body/eval_jaxpr/thn,shn->hts/dot_general | solution.py:60
  171.5 6.5 fusion.123
  178.0 7.3 %fusion.124 = f32[128,32,64]{0,2,1:T(8,128)S(1)} fusion(f32[128,32,64]{0,2,1:T(8,128)} %fusion.123, f32[32,64,256]{2,1,0:T(8,128)S(1)} %get-tuple-element.291, f32[512,32,256]{2,0,1:T(8,128)} %get-tuple-element.312, s32[]{:T(128)S(6)} %select_n.102, pred[]{:T(512)S(6)} %compare.7, f32[128,32]{0,1:T(8,128)S(1)} %get-tuple-element.275), kind=kOutput, calls=%fused_computation.23.clone.1 | convolution fusion | flops 806354944 | bytes 8404997 | tf_op jit(solution)/shard_map/while/body/eval_jaxpr/thn,hpn->thp/dot_general | solution.py:63
  185.2 26.4 %dynamic_update_slice.6 = f32[4,128,32,64]{1,0,3,2:T(4,128)} dynamic-update-slice(f32[4,128,32,64]{1,0,3,2:T(4,128)} %get-tuple-element.292, f32[1,128,32,64]{1,0,3,2:T(1,128)S(1)} %bitcast.82, s32[]{:T(128)} %get-tuple-element.290, s32[]{:T(128)} %constant.87.clone.1..sunk.1, s32[]{:T(128)} %constant.87.clone.1..sunk.1, s32[]{:T(128)} %constant.87.clone.1..sunk.1) | dynamic-update-slice | bytes 2097156 | tf_op jit(solution)/shard_map/while/body/jit(dynamic_update_index_in_dim)/dynamic_update_slice | solution.py:151
  211.7 5.7 multiply_add_fusion.4
  217.4 0.6 dynamic_slice.123
  218.6 0.3 reduce_window_sum.33
  219.2 7.9 %fusion.122 = f32[32,128,128]{2,1,0:T(8,128)S(1)} fusion(f32[512,32,256]{2,0,1:T(8,128)} %get-tuple-element.312, s32[]{:T(128)S(6)} %select_n.102, f32[512,32,256]{2,0,1:T(8,128)} %get-tuple-element.311), kind=kOutput, calls=%fused_computation.6.clone.1 | convolution fusion | flops 1610612736 | bytes 10486784 | tf_op jit(solution)/shard_map/while/body/eval_jaxpr/thn,shn->hts/dot_general | solution.py:60
  227.1 6.5 fusion.123
  233.6 7.3 %fusion.124 = f32[128,32,64]{0,2,1:T(8,128)S(1)} fusion(f32[128,32,64]{0,2,1:T(8,128)} %fusion.123, f32[32,64,256]{2,1,0:T(8,128)S(1)} %get-tuple-element.291, f32[512,32,256]{2,0,1:T(8,128)} %get-tuple-element.312, s32[]{:T(128)S(6)} %select_n.102, pred[]{:T(512)S(6)} %compare.7, f32[128,32]{0,1:T(8,128)S(1)} %get-tuple-element.275), kind=kOutput, calls=%fused_computation.23.clone.1 | convolution fusion | flops 806354944 | bytes 8404997 | tf_op jit(solution)/shard_map/while/body/eval_jaxpr/thn,hpn->thp/dot_general | solution.py:63
  240.9 26.4 %dynamic_update_slice.6 = f32[4,128,32,64]{1,0,3,2:T(4,128)} dynamic-update-slice(f32[4,128,32,64]{1,0,3,2:T(4,128)} %get-tuple-element.292, f32[1,128,32,64]{1,0,3,2:T(1,128)S(1)} %bitcast.82, s32[]{:T(128)} %get-tuple-element.290, s32[]{:T(128)} %constant.87.clone.1..sunk.1, s32[]{:T(128)} %constant.87.clone.1..sunk.1, s32[]{:T(128)} %constant.87.clone.1..sunk.1) | dynamic-update-slice | bytes 2097156 | tf_op jit(solution)/shard_map/while/body/jit(dynamic_update_index_in_dim)/dynamic_update_slice | solution.py:151
  267.3 5.7 multiply_add_fusion.4
  273.2 1.1 convert_element_type.73
  274.4 0.7 all-gather.5.cloned.1.call-update
  275.2 1.2 reduce-window.6
  276.6 0.6 dynamic-slice
  278.1 0.2 dynamic-update-slice
  278.4 5.7 all-reduce
  284.3 5.5 reshape.133
  289.8 19.6 %all-gather.7.cloned.1.call-done = bf16[128,64,256]{2,1,0:T(8,128)(2,1)} async-done(((bf16[32,64,256]{2,1,0:T(8,128)(2,1)}), bf16[128,64,256]{2,1,0:T(8,128)(2,1)}) %all-gather.7.cloned.1.call-update) | async-done | bytes 4194320 | tf_op jit(solution)/shard_map/all_gather | solution.py:28
  309.3 1.6 broadcast_in_dim.39
  310.9 1.0 copy-done.2
  311.9 20.5 %fusion.68 = f32[512,32,64]{0,2,1:T(8,128)} fusion(f32[512,32,64]{0,2,1:T(8,128)} %reshape.133, f32[512,32,64]{0,2,1:T(8,128)} %get-tuple-element.348, f32[512,256]{1,0:T(8,128)S(1)} %copy-done.2, f32[32]{0:T(128)S(1)} %copy-done.6, f32[512,32]{0,1:T(8,128)S(1)} %exponential_bitcast_fusion.1, f32[32,64,256]{2,1,0:T(8,128)} %get-tuple-element.87, ...), kind=kOutput, calls=%fused_computation.70 | convolution fusion | flops 3226468352 | bytes 17367296 | tf_op jit(solution)/shard_map/thn,hpn->thp/dot_general | solution.py:164
  332.4 5.9 copy.36
  338.3 4.8 multiply_reduce_fusion
  343.1 37.3 %psum.7 = f32[8,512]{1,0:T(8,128)S(1)} all-reduce(f32[8,512]{1,0:T(8,128)S(1)} %broadcast_multiply_fusion.1), channel_id=1, replica_groups=mesh['seq'=4,'head'=8] {'head'}, use_global_device_ids=true, to_apply=%region_8.9 | all-reduce | flops 4096 | bytes 32768 | tf_op jit(solution)/shard_map/psum | solution.py:180
  380.5 132.0 %all-gather.5.cloned.1.call-done = bf16[2048,8192]{1,0:T(8,128)(2,1)} async-done(((bf16[2048,2048]{1,0:T(8,128)(2,1)}), bf16[2048,8192]{1,0:T(8,128)(2,1)}) %all-gather.5.cloned.1.call-update) | async-done | bytes 33554448 | tf_op jit(solution)/shard_map/all_gather | solution.py:188
  512.5 28.9 %convolution_convert_fusion = bf16[512,8192]{1,0:T(8,128)(2,1)} fusion(bf16[2048,8192]{1,0:T(8,128)(2,1)} %all-gather.5.cloned.1.call-done, f32[2048]{0:T(1024)S(1)} %copy-done.7, f32[512]{0:T(512)S(1)} %add_rsqrt_fusion, f32[512,2048]{1,0:T(8,128)} %copy.36, bf16[512,2048]{1,0:T(8,128)(2,1)} %param.20), kind=kOutput, calls=%fused_computation.47 | convolution fusion | flops 17193500672 | bytes 48244736 | tf_op jit(solution)/shard_map/dot_general | solution.py:186
  541.6 4.0 add_bitcast_fusion
  545.6 145.0 %reduce-scatter.2.cloned.1.call-done = bf16[64,8192]{1,0:T(8,128)(2,1)} async-done(((bf16[512,8192]{1,0:T(8,128)(2,1)}), bf16[64,8192]{1,0:T(8,128)(2,1)}) %reduce-scatter.2.cloned.1.call-update) | async-done | bytes 1048592 | tf_op jit(solution)/shard_map/reduce_scatter | solution.py:191
  (70 shorter events, 2.7 us)
Async XLA Ops:
  7.2 302.2 %all-gather.7.cloned.1.call-start = ((), (), s32[]{:S(2)}) async-start(), calls=%async_computation.3 | async-start | bytes 5242880 | tf_op jit(solution)/shard_map/all_gather | solution.py:28
  7.2 13.8 %copy-start.3 = (bf16[512,2048]{1,0:T(8,128)(2,1)S(1)}, bf16[512,2048]{1,0:T(8,128)(2,1)}, u32[]{:S(2)}) copy-start(bf16[512,2048]{1,0:T(8,128)(2,1)} %param.19) | copy-start | bytes 6291460
  8.5 15.0 %collective-permute-start.1 = (bf16[3,512]{1,0:T(4,128)(2,1)S(1)}, bf16[3,512]{1,0:T(4,128)(2,1)S(1)}, u32[]{:S(2)}, u32[]{:S(2)}) collective-permute-start(bf16[3,512]{1,0:T(4,128)(2,1)S(1)} %fusion.86), channel_id=1, source_target_pairs={{0,8},{8,16},{16,24},{1,9},{9,17},{17,25},{2,10},{10,18},{18,26},{... | collective-permute-start | bytes 9224 | tf_op jit(solution)/shard_map/ppermute | solution.py:22
  11.6 12.7 %collective-permute-start = (bf16[3,2048]{1,0:T(4,128)(2,1)S(1)}, bf16[3,2048]{1,0:T(4,128)(2,1)S(1)}, u32[]{:S(2)}, u32[]{:S(2)}) collective-permute-start(bf16[3,2048]{1,0:T(4,128)(2,1)S(1)} %slice.68), channel_id=1, source_target_pairs={{0,8},{8,16},{16,24},{1,9},{9,17},{17,25},{2,10},{10,18},{18,26},{... | collective-permute-start | bytes 36872 | tf_op jit(solution)/shard_map/ppermute | solution.py:22
  21.0 3.3 copy-start.4
  21.0 3.3 copy-start.5
  23.5 2.4 copy-start
  24.3 18.6 %copy-start.1 = (f32[512,256]{1,0:T(8,128)}, f32[512,256]{1,0:T(8,128)S(1)}, u32[]{:S(2)}) copy-start(f32[512,256]{1,0:T(8,128)S(1)} %get-tuple-element.155) | copy-start | bytes 1572868
  274.4 2.2 copy-start.8
  274.4 238.1 %all-gather.5.cloned.1.call-start = ((), (), s32[]{:S(2)}) async-start(), calls=%async_computation.1 | async-start | bytes 41943040 | tf_op jit(solution)/shard_map/all_gather | solution.py:188
  275.1 415.5 %reduce-scatter.2.cloned.1.call-start = ((), (), s32[]{:S(2)}) async-start(), calls=%async_computation.2 | async-start | bytes 9437184 | tf_op jit(solution)/shard_map/reduce_scatter | solution.py:191
  310.9 1.0 copy-start.2
  310.9 1.0 copy-start.6
  338.3 174.2 %copy-start.7 = (f32[2048]{0:T(1024)S(1)}, f32[2048]{0:T(1024)}, u32[]{:S(2)}) copy-start(f32[2048]{0:T(1024)} %param.32) | copy-start | bytes 24580
Sparse Core Ops, SparseCore 0:
  274.5 34.7 all-gather.6
  310.9 201.5 all-gather.4
  541.5 149.0 reduce-scatter.1
where the time goes:
time: 701 us; the launch traced here: 697 us
  waiting for transfers between devices  297 us (42%)
  matrix products  159 us (23%)
  local copies, waits for them, and re-layouts  152 us (22%)
  blocking collectives  43 us (6%)
  other arithmetic  21.7 us (3%)
  between operations  14.6 us (2%)
    reduce_scatter x1, waiting for transfers between devices, body(): lax.psum_scatter(terms.astype(jnp.bfloat16), 'head', scatter_dimension=0,...  145 us
    all_gather x1, waiting for transfers between devices, body(): lax.all_gather(out_weight, 'seq', axis=1, tiled=True)  132 us
    dynamic_update_slice x4, local copies, waits for them, and re-layouts, body(): lax.scan(span_step_body, empty_state, jnp.arange(spans_here, dtype=jnp.in...  106 us
    psum x1, blocking collectives, body(): group_totals = lax.psum(contribution, 'head')  37.3 us
    dot_general x4, matrix products, ssd_block(): scores = jnp.einsum('thn,shn->hts', span_c, span_b, precision=highest)  31.5 us
    dot_general x4, matrix products, ssd_block(): carried = jnp.einsum('thn,hpn->thp', span_c, state, precision=highest)  29.1 us
    dot_general x1, matrix products, body(): jnp.dot(normed, lax.all_gather(out_weight, 'seq', axis=1, tiled=True), pr...  28.9 us
    dot_general x4, matrix products, ssd_block(): output = jnp.einsum('hts,shp->thp', mixer, span_x, precision=highest)  26.1 us
  transfers between devices with their start and end apart: 5, of which 3 were waited for; matrix products, arithmetic and copies ran while one was open for 8% of the time, Pallas kernels for 0%

commit v1 on v0

v1 whole, which is shorter than its diff:
```python
import functools

import jax
import jax.numpy as jnp
from jax import lax
from jax.experimental import pallas as pl
from jax.experimental.pallas import tpu as pltpu
from jax.sharding import PartitionSpec as P

MIXER_HEADS = 256
HEADDIM = 64
STATE = 256
GROUPS = 8
KERNEL = 4
SPAN = 128
DINNER = 16384
EXTRA = 16
VMEM_LIMIT = 48 * 1024 * 1024

highest = lax.Precision.HIGHEST
norm_eps = 1e-05
f32 = jnp.float32
bf16 = jnp.bfloat16


def silu(v):
    return v * (1.0 / (1.0 + jnp.exp(-v)))


def shifted(cur, prev8, by):
    moved = pltpu.roll(cur, by, 0)
    before = pltpu.roll(prev8, by, 0)
    row = lax.broadcasted_iota(jnp.int32, before.shape, 0)
    first = jnp.where(row < by, before, moved[:8])
    return jnp.concatenate([first, moved[8:]], axis=0)


def conv_block(in_ref, prev_ref, w_ref, b_ref, out_ref, chunk):
    width = in_ref.shape[1]
    rows = in_ref.shape[0]
    for c in range(0, width, chunk):
        cols = slice(c, c + chunk)
        cur = in_ref[:, cols].astype(f32)
        prev8 = prev_ref[:, cols]
        total = b_ref[:, cols] + w_ref[KERNEL - 1 : KERNEL, cols] * cur
        for by in range(1, KERNEL):
            k = KERNEL - 1 - by
            total = total + w_ref[k : k + 1, cols] * shifted(cur, prev8, by)
        prev_ref[:, cols] = cur[rows - 8 :]
        out_ref[:, cols] = silu(total).astype(bf16)


def spread_matrix(heads):
    h = lax.broadcasted_iota(jnp.int32, (heads, heads * HEADDIM), 0)
    c = lax.broadcasted_iota(jnp.int32, (heads, heads * HEADDIM), 1)
    return jnp.where(c // HEADDIM == h, 1.0, 0.0).astype(f32)


def spread(values, matrix):
    return jnp.dot(values, matrix, precision=highest, preferred_element_type=f32)


def softplus(v):
    e = jnp.exp(-jnp.abs(v))
    u = 1.0 + e
    series = e * (1.0 - e * (0.5 - e * (1.0 / 3.0 - 0.25 * e)))
    return jnp.maximum(v, 0.0) + jnp.where(e < 0.015625, series, jnp.log(u))


def transposed_dot(lhs, rhs):
    return lax.dot_general(
        lhs, rhs, (((1,), (1,)), ((), ())), precision=highest, preferred_element_type=f32
    )


def decay_terms(dt_ref, rate_ref):
    step = softplus(dt_ref[...])
    log = -jnp.exp(rate_ref[...]) * step
    t = lax.broadcasted_iota(jnp.int32, (SPAN, SPAN), 0)
    s = lax.broadcasted_iota(jnp.int32, (SPAN, SPAN), 1)
    lower = jnp.where(t >= s, 1.0, 0.0).astype(f32)
    eye = jnp.where(t == s, 1.0, 0.0).astype(f32)
    cumul_row = transposed_dot(log, lower)
    cumul_col = transposed_dot(lower, log)
    step_col = transposed_dot(eye, step)
    return step, step_col, cumul_row, cumul_col, t >= s


def state_kernel(
    g_ref, inner, bin_, cin, dt, rate, wx, bx, wb, wc, bb, bc, halo_x, halo_b, halo_c,
    x_out, b_out, c_out, enter_out, send_out, local_out,
    prev_x, prev_b, prev_c, state, total,
):
    i = pl.program_id(0)
    heads = dt.shape[0]

    @pl.when(i == 0)
    def _():
        prev_x[...] = halo_x[...].astype(f32)
        prev_b[...] = halo_b[...].astype(f32)
        prev_c[...] = halo_c[...].astype(f32)
        state[...] = jnp.zeros_like(state)
        total[...] = jnp.zeros_like(total)

    conv_block(inner, prev_x, wx, bx, x_out, 256)
    conv_block(bin_, prev_b, wb, bb, b_out, 256)
    conv_block(cin, prev_c, wc, bc, c_out, 256)
    step, step_col, cumul_row, cumul_col, causal = decay_terms(dt, rate)
    last = cumul_col[SPAN - 1 :]
    matrix = spread_matrix(heads)
    weights = spread(jnp.exp(last - cumul_col) * step_col, matrix)
    last8 = spread(jnp.broadcast_to(last, (8, heads)), matrix)
    enter_out[0] = state[...].astype(bf16)
    weighted = (x_out[...].astype(f32) * weights).astype(bf16)
    b_t = b_out[...].astype(f32).T.astype(bf16)
    written = jnp.dot(b_t, weighted, preferred_element_type=f32)
    state[...] = jnp.exp(last8[:1]) * state[...] + written
    total[...] += last8

    @pl.when(i == pl.num_programs(0) - 1)
    def _():
        local_out[...] = state[...]
        send_out[:STATE] = state[...].astype(bf16)
        tl = total[:1]
        high = tl.astype(bf16).astype(f32)
        row = lax.broadcasted_iota(jnp.int32, (EXTRA, tl.shape[1]), 0)
        send_out[STATE:] = jnp.where(row == 0, high, jnp.where(row == 1, tl - high, 0.0)).astype(bf16)


def local_kernel(x, b, c, dt, rate, skip, enter, y_out):
    heads = dt.shape[0]
    step, step_col, cumul_row, cumul_col, causal = decay_terms(dt, rate)
    matrix = spread_matrix(heads)
    scores = lax.dot_general(
        c[...], b[...], (((1,), (1,)), ((), ())), preferred_element_type=f32
    )
    row_term = jnp.log(step) - cumul_row
    growth = spread(jnp.exp(cumul_col), matrix)
    skip_row = spread(jnp.broadcast_to(skip[...], (8, heads)), matrix)[:1]
    lane = lax.broadcasted_iota(jnp.int32, (SPAN, 2 * HEADDIM), 1)
    zero = jnp.zeros((SPAN, 2 * HEADDIM), bf16)
    for pair in range(heads // 2):
        cols = slice(pair * 2 * HEADDIM, (pair + 1) * 2 * HEADDIM)
        mixers = []
        for h in (2 * pair, 2 * pair + 1):
            power = jnp.where(causal, cumul_col[:, h : h + 1] + row_term[h : h + 1], -1e30)
            mixers.append((scores * jnp.exp(power)).astype(bf16))
        xp = x[:, cols]
        both = jnp.concatenate(
            [jnp.where(lane < HEADDIM, xp, zero), jnp.where(lane >= HEADDIM, xp, zero)], axis=0
        )
        inside = jnp.dot(
            jnp.concatenate(mixers, axis=1), both, preferred_element_type=f32
        )
        carried = jnp.dot(c[...], enter[0, :, cols], preferred_element_type=f32)
        y_out[:, cols] = (
            inside + growth[:, cols] * carried + skip_row[:, cols] * xp.astype(f32)
        )


def output_kernel(
    meta, y, c, gate, dt, rate, gain, gathered, init, local, normed_out, boundary_out,
    incoming, entering, mixed, offset, *, block, whole_group,
):
    i = pl.program_id(0)
    heads = dt.shape[0]
    width = y.shape[1]
    count = gathered.shape[0]

    @pl.when(i == 0)
    def _():
        place = meta[0]
        rate_sum = jnp.zeros((1, width), f32)
        incoming[...] = jnp.zeros_like(incoming)
        for k in range(count - 2, -1, -1):
            live = k < place
            tail = gathered[k, STATE:].astype(f32)
            factor = jnp.where(live, jnp.exp(rate_sum), 0.0)
            incoming[...] += factor * gathered[k, :STATE].astype(f32)
            rate_sum = rate_sum + jnp.where(live, tail[0:1] + tail[1:2], 0.0)
        tail = gathered[place, STATE:].astype(f32)
        own = jnp.exp(tail[0:1] + tail[1:2])
        for k in range(0, width, 256):
            cols = slice(k, k + 256)
            value = incoming[:, cols] + jnp.exp(rate_sum[:, cols]) * init[cols, :].T
            entering[:, cols] = value.astype(bf16)
            boundary_out[cols, :] = (own[:, cols] * value + local[:, cols]).T
        offset[...] = jnp.zeros_like(offset)

    step, step_col, cumul_row, cumul_col, causal = decay_terms(dt, rate)
    cumul_col = cumul_col + offset[:1]
    offset[...] = jnp.broadcast_to(cumul_col[SPAN - 1 :], offset.shape)
    growth = spread(jnp.exp(cumul_col), spread_matrix(heads))
    squares = jnp.zeros((SPAN, 1), f32)
    for k in range(0, width, 256):
        cols = slice(k, k + 256)
        carried = jnp.dot(c[...], entering[:, cols], preferred_element_type=f32)
        value = (y[:, cols] + growth[:, cols] * carried) * silu(gate[:, cols].astype(f32))
        mixed[:, cols] = value
        squares = squares + jnp.sum(value * value, axis=1, keepdims=True)
    if whole_group:
        inverse = lax.rsqrt(squares / width + norm_eps)
    for q in range(SPAN // block):
        rows = slice(q * block, (q + 1) * block)
        place = pl.multiple_of(meta[1 + i * (SPAN // block) + q], block)
        value = mixed[rows, :]
        if whole_group:
            value = value * inverse[rows] * gain[...]
        normed_out[pl.ds(place, block), :] = value.astype(normed_out.dtype)


def params():
    return pltpu.CompilerParams(vmem_limit_bytes=VMEM_LIMIT)


def body(
    inner_input,
    gate_input,
    bc_input,
    dt_input,
    log_rate,
    skip_weight,
    conv_weight_x,
    conv_bias_x,
    conv_weight_bc,
    conv_bias_bc,
    conv_tail_x,
    conv_tail_bc,
    init_state,
    norm_gain,
    out_weight,
):
    seq_count = lax.axis_size("seq")
    head_count = lax.axis_size("head")
    seq_index = lax.axis_index("seq")
    head_index = lax.axis_index("head")
    rows, width = inner_input.shape
    heads = dt_input.shape[0]
    per_group = MIXER_HEADS // GROUPS
    group = (head_index * heads // per_group).astype(jnp.int32)
    spans = rows // SPAN
    block = rows // head_count
    group_width = DINNER // GROUPS
    whole_group = width == group_width

    other_core = lax.ppermute(out_weight, "seq", [(i, i ^ 1) for i in range(seq_count)])

    def pair_columns(table, axis):
        return [
            lax.dynamic_slice_in_dim(table, (g + group) * STATE, STATE, axis) for g in (0, GROUPS)
        ]

    tail_rows = rows - KERNEL + 1
    last_rows = jnp.concatenate(
        [inner_input[tail_rows:]] + pair_columns(bc_input[tail_rows:], 1), axis=1
    )
    arrived = lax.ppermute(last_rows, "seq", [(i, i + 1) for i in range(seq_count - 1)])
    first_rows = jnp.concatenate([conv_tail_x] + pair_columns(conv_tail_bc, 1), axis=1)
    halo = jnp.where(seq_index == 0, first_rows, arrived)
    halo = jnp.pad(halo, ((8 - KERNEL + 1, 0), (0, 0)))
    rate = log_rate[:, None]

    def const(shape, *index):
        return pl.BlockSpec(shape, lambda i, *_: index)

    span_x = pl.BlockSpec((SPAN, width), lambda i, *_: (i, 0))
    span_bc = pl.BlockSpec((SPAN, STATE), lambda i, *_: (i, 0))
    span_dt = pl.BlockSpec((heads, SPAN), lambda i, *_: (0, i))

    conv_x, conv_b, conv_c, enter, sent, local = pl.pallas_call(
        state_kernel,
        grid_spec=pltpu.PrefetchScalarGridSpec(
            num_scalar_prefetch=1,
            grid=(spans,),
            in_specs=[
                span_x,
                pl.BlockSpec((SPAN, STATE), lambda i, g: (i, g[0])),
                pl.BlockSpec((SPAN, STATE), lambda i, g: (i, g[0] + GROUPS)),
                span_dt,
                const((heads, 1), 0, 0),
                const((KERNEL, width), 0, 0),
                const((1, width), 0, 0),
                pl.BlockSpec((KERNEL, STATE), lambda i, g: (0, g[0])),
                pl.BlockSpec((KERNEL, STATE), lambda i, g: (0, g[0] + GROUPS)),
                pl.BlockSpec((1, STATE), lambda i, g: (0, g[0])),
                pl.BlockSpec((1, STATE), lambda i, g: (0, g[0] + GROUPS)),
                const((8, width), 0, 0),
                const((8, STATE), 0, width // STATE),
                const((8, STATE), 0, width // STATE + 1),
            ],
            out_specs=[
                span_x,
                span_bc,
                span_bc,
                pl.BlockSpec((1, STATE, width), lambda i, *_: (i, 0, 0)),
                const((STATE + EXTRA, width), 0, 0),
                const((STATE, width), 0, 0),
            ],
            scratch_shapes=[
                pltpu.VMEM((8, width), f32),
                pltpu.VMEM((8, STATE), f32),
                pltpu.VMEM((8, STATE), f32),
                pltpu.VMEM((STATE, width), f32),
                pltpu.VMEM((8, width), f32),
            ],
        ),
        out_shape=[
            jax.ShapeDtypeStruct((rows, width), bf16),
            jax.ShapeDtypeStruct((rows, STATE), bf16),
            jax.ShapeDtypeStruct((rows, STATE), bf16),
            jax.ShapeDtypeStruct((spans, STATE, width), bf16),
            jax.ShapeDtypeStruct((STATE + EXTRA, width), bf16),
            jax.ShapeDtypeStruct((STATE, width), f32),
        ],
        compiler_params=params(),
        name="conv_and_states",
    )(
        group[None],
        inner_input, bc_input, bc_input, dt_input, rate,
        conv_weight_x, conv_bias_x[None], conv_weight_bc, conv_weight_bc,
        conv_bias_bc[None], conv_bias_bc[None], halo, halo, halo,
    )

    gathered = lax.all_gather(sent, "seq")

    y_local = pl.pallas_call(
        local_kernel,
        grid=(spans,),
        in_specs=[
            span_x,
            span_bc,
            span_bc,
            span_dt,
            const((heads, 1), 0, 0),
            const((1, heads), 0, 0),
            pl.BlockSpec((1, STATE, width), lambda i: (i, 0, 0)),
        ],
        out_specs=span_x,
        out_shape=jax.ShapeDtypeStruct((rows, width), f32),
        compiler_params=params(),
        cost_estimate=pl.CostEstimate(
            flops=4 * rows * width * STATE, bytes_accessed=rows * width * 8, transcendentals=0
        ),
        name="local_outputs",
    )(conv_x, conv_b, conv_c, dt_input, rate, skip_weight[None], enter)

    bits = head_count.bit_length() - 1
    distance = jnp.arange(head_count, dtype=jnp.int32) ^ head_index
    slot = jnp.zeros_like(distance)
    for bit in range(bits):
        slot = slot + ((distance >> bit) & 1) * (head_count >> (bit + 1))
    meta = jnp.concatenate([seq_index[None].astype(jnp.int32), slot.astype(jnp.int32) * block])

    normed, boundary = pl.pallas_call(
        functools.partial(output_kernel, block=block, whole_group=whole_group),
        grid_spec=pltpu.PrefetchScalarGridSpec(
            num_scalar_prefetch=1,
            grid=(spans,),
            in_specs=[
                span_x,
                span_bc,
                span_x,
                span_dt,
                const((heads, 1), 0, 0),
                const((1, width), 0, 0),
                const((seq_count, STATE + EXTRA, width), 0, 0, 0),
                const((width, STATE), 0, 0),
                const((STATE, width), 0, 0),
            ],
            out_specs=[const((rows, width), 0, 0), const((width, STATE), 0, 0)],
            scratch_shapes=[
                pltpu.VMEM((STATE, width), f32),
                pltpu.VMEM((STATE, width), bf16),
                pltpu.VMEM((SPAN, width), f32),
                pltpu.VMEM((8, heads), f32),
            ],
        ),
        out_shape=[
            jax.ShapeDtypeStruct((rows, width), bf16 if whole_group else f32),
            jax.ShapeDtypeStruct((width, STATE), f32),
        ],
        compiler_params=params(),
        name="gated_outputs",
    )(
        meta,
        y_local, conv_c, gate_input, dt_input, rate, norm_gain[None], gathered,
        init_state.reshape(width, STATE), local,
    )
    boundary = boundary.reshape(1, heads, HEADDIM, STATE)

    if not whole_group:
        piece = min(width, group_width)
        pieces = normed.reshape(rows, width // piece, piece)
        squares = jnp.sum(pieces * pieces, axis=2).T
        blocks = squares.reshape(squares.shape[0], head_count, block)
        ordered = jnp.take(blocks, slot, axis=1).reshape(squares.shape)
        own = (head_index * (width // piece) + jnp.arange(width // piece)) * piece // group_width
        member = (own[:, None] == jnp.arange(GROUPS)[None, :]).astype(f32)
        totals = lax.psum(jnp.dot(member.T, ordered, precision=highest), "head")
        sums = jnp.dot(member, totals, precision=highest)
        inverse = lax.rsqrt(sums / group_width + norm_eps)
        back = jnp.zeros_like(slot).at[slot].set(jnp.arange(head_count, dtype=slot.dtype))
        inverse = jnp.take(inverse.reshape(blocks.shape), back, axis=1).reshape(squares.shape).T
        normed = (
            (pieces * inverse[:, :, None]).reshape(rows, width) * norm_gain[None, :]
        ).astype(bf16)

    chips = seq_count // 2

    def around(value, by):
        if by % chips == 0:
            return value
        return lax.ppermute(
            value, "seq", [(i, (i + 2 * by) % seq_count) for i in range(seq_count)]
        )

    def across(value, bit):
        return lax.ppermute(
            value, "head", [(i, i ^ (1 << bit)) for i in range(head_count)]
        )

    def reduced(act, weight):
        half = rows // 2
        give = jnp.dot(act[half:], weight, preferred_element_type=f32).astype(bf16)
        keep = jnp.dot(act[:half], weight, preferred_element_type=f32)
        keep = keep + across(give, 0).astype(f32)
        for bit in range(1, bits):
            half = half // 2
            got = across(keep[half:].astype(bf16), bit)
            keep = keep[:half] + got.astype(f32)
        return keep.astype(bf16)

    core = seq_index % 2
    columns = out_weight.shape[1]
    layer_out = jnp.zeros((block, seq_count, columns), bf16)
    acts = [around(normed, by) for by in range(chips)]
    done = [[reduced(act, w) for w in (out_weight, other_core)] for act in acts]
    for by in range(chips):
        mine, other = [around(d, -by) for d in done[by]]
        chip = (seq_index // 2 + by) % chips
        layer_out = lax.dynamic_update_slice(
            layer_out, mine[:, None], (0, chip * 2 + core, 0)
        )
        layer_out = lax.dynamic_update_slice(
            layer_out, other[:, None], (0, chip * 2 + 1 - core, 0)
        )
    return (layer_out.reshape(block, seq_count * columns), boundary)


def solution(mesh):
    in_specs = (
        P("seq", "head"),
        P("seq", "head"),
        P("seq", None),
        P("head", "seq"),
        P("head"),
        P("head"),
        P(None, "head"),
        P("head"),
        P(),
        P(),
        P(None, "head"),
        P(),
        P("head", None, None),
        P("head"),
        P("head", "seq"),
    )
    out_specs = (P(("seq", "head"), None), P("seq", "head", None, None))
    return jax.shard_map(body, mesh=mesh, in_specs=in_specs, out_specs=out_specs, check_vma=False)
```

time: 701 us -> 289 us (0.41)
  waiting for transfers between devices: 297 us -> 140 us
  local copies, waits for them, and re-layouts: 152 us -> 28.6 us
  matrix products: 159 us -> 44.8 us
  blocking collectives: 43 us -> 0 us
  Pallas kernels: 0 us -> 37.7 us
  other arithmetic: 21.7 us -> 1.49 us
  starting transfers between devices: 6.98 us -> 21.3 us
    reduce_scatter x1 -> x0, waiting for transfers between devices: 145 us -> none  [body(): lax.psum_scatter(terms.astype(jnp.bfloat16), 'head', scatter_dimension=0,...]
    all_gather x2 -> x1, waiting for transfers between devices: 152 us -> 25.3 us  [body(): gathered = lax.all_gather(sent, 'seq')]
    ppermute x2 -> x17, waiting for transfers between devices: 0.01 us -> 115 us  [the longest x12 94.3 us: across(): lax.ppermute(value, 'head', [(i, i ^ 1 << bit) for i in range(head_count)])]
    dot_general x19 -> x8, matrix products: 159 us -> 44.8 us  [the longest x4 25.4 us: reduced(): give = jnp.dot(act[half:], weight, preferred_element_type=f32).astype(bf16)]
    dynamic_update_slice x4, local copies, waits for them, and re-layouts: 106 us -> 13.3 us  [the longest x2 6.76 us: body(): lax.dynamic_update_slice(layer_out, mine[:, None], (0, chip * 2 + core, 0))]
    pallas_call x0 -> x3, Pallas kernels: none -> 37.7 us  [the longest x1 14.9 us: body(): pl.pallas_call(functools.partial(output_kernel, block=block, whole_group=...]
    psum x1 -> x0, blocking collectives: 37.3 us -> none  [body(): group_totals = lax.psum(contribution, 'head')]
    reshape x6 -> x0, local copies, waits for them, and re-layouts: 31.9 us -> none  [the longest x1 7.6 us: body(): jnp.repeat(bc_float[:, :width_bc].reshape(row_count, groups_here, STATE),...]
  transfers between devices with their start and end apart: 5 -> 18, of which waited for: 3 -> 10; matrix products, arithmetic and copies ran while one was open for 8% -> 19% of each run, Pallas kernels for 0% -> 9%
where the time goes in v1:
time: 289 us
  waiting for transfers between devices  140 us (48%)
  matrix products  44.8 us (16%)
  Pallas kernels  37.7 us (13%)
  local copies, waits for them, and re-layouts  28.6 us (10%)
  starting transfers between devices  21.3 us (7%)
  between operations  14.4 us (5%)
    ppermute x12, waiting for transfers between devices, across(): lax.ppermute(value, 'head', [(i, i ^ 1 << bit) for i in range(head_count)])  94.3 us
    dot_general x4, matrix products, reduced(): give = jnp.dot(act[half:], weight, preferred_element_type=f32).astype(bf16)  25.4 us
    all_gather x1, waiting for transfers between devices, body(): gathered = lax.all_gather(sent, 'seq')  25.3 us
    ppermute x3, waiting for transfers between devices, around(): lax.ppermute(value, 'seq', [(i, (i + 2 * by) % seq_count) for i in range(...  20.7 us
    dot_general x4, matrix products, reduced(): keep = jnp.dot(act[:half], weight, preferred_element_type=f32)  19.3 us
    pallas_call x1, Pallas kernels, body(): pl.pallas_call(functools.partial(output_kernel, block=block, whole_group=...  14.9 us
    ppermute x12, starting transfers between devices, across(): lax.ppermute(value, 'head', [(i, i ^ 1 << bit) for i in range(head_count)])  14.4 us
    pallas_call x1, Pallas kernels, body(): pl.pallas_call(state_kernel, grid_spec=pltpu.PrefetchScalarGridSpec(num_s...  12.4 us
  transfers between devices with their start and end apart: 18, of which 10 were waited for; matrix products, arithmetic and copies ran while one was open for 19% of the time, Pallas kernels for 9%

profile of v1, /device:TPU:0, one launch (start us, length us, event | category | flops | bytes accessed | tf_op | source)
XLA Modules:
  0.0 288.7 jit_solution(10667543886407445155)
XLA Ops:
  7.2 0.9 slice.79
  8.1 0.8 slice.78
  8.9 2.4 collective-permute-start
  11.3 0.7 constant_dynamic-slice_fusion.3
  12.0 0.7 copy.17.rate
  12.7 0.7 maximum_select_fusion
  13.5 0.8 copy-done.4
  14.4 0.8 copy-done.6
  15.2 0.7 copy-done.7
  15.9 0.8 copy-done.8
  16.7 0.7 copy-done.10
  17.4 12.4 %conv_and_states.1 = (bf16[512,2048]{1,0:T(8,128)(2,1)S(1)}, bf16[512,256]{1,0:T(8,128)(2,1)S(1)}, bf16[512,256]{1,0:T(8,128)(2,1)S(1)}, bf16[4,256,2048]{2,1,0:...) custom-call(s32[1]{0:T(128)} %bitcast.1.g_ref, bf16[512,2048]{1,0:T(8,128)(2,1)} %inner.1, ...), custom_call_target="tpu_custom_call" | custom-call | tf_op jit(solution)/shard_map/conv_and_states/pallas_call | solution.py:270
  29.8 1.3 copy-done.1
  31.1 1.3 copy-done.2
  32.5 2.7 collective-permute-start.4
  35.2 1.6 copy-done.3
  36.8 10.4 %local_outputs.1.y = f32[512,2048]{1,0:T(8,128)} custom-call(bf16[512,2048]{1,0:T(8,128)(2,1)S(1)} %copy-done.3, bf16[512,256]{1,0:T(8,128)(2,1)S(1)} %get-tuple-element.11.b, bf16[512,256]{1,0:T(8,128)(2,1)S(1)} %get-tuple-element.12.c, f32[32,512]{1,0:T(8,128)S(1)} %copy-done.5, f32[32,1]{1,0:T(8,128)S(1)} %copy.17.rate, f32[1,32]{1,0:T(1,128)S(1)} %bitcast.30, ...), custom_call_target="tpu_custom_call" | custom-call | flops 1073741824 | bytes 8388608 | tf_op jit(solution)/shard_map/local_outputs/pallas_call | solution.py:326
  47.3 25.3 %all-gather.3.cloned.1.call-done = bf16[1088,2048]{1,0:T(8,128)(2,1)} async-done(((bf16[272,2048]{1,0:T(8,128)(2,1)}), bf16[1088,2048]{1,0:T(8,128)(2,1)}) %all-gather.3.cloned.1.call-update) | async-done | bytes 4456464 | tf_op jit(solution)/shard_map/all_gather | solution.py:324
  72.6 14.9 %gated_outputs.1 = (bf16[512,2048]{1,0:T(8,128)(2,1)}, f32[2048,256]{1,0:T(8,128)}) custom-call(s32[9]{0:T(128)S(1)} %pad_add_fusion.meta, f32[512,2048]{1,0:T(8,128)} %local_outputs.1.y, bf16[512,256]{1,0:T(8,128)(2,1)S(1)} %get-tuple-element.12.c, bf16[512,2048]{1,0:T(8,128)(2,1)S(1)} %copy-done, f32[32,512]{1,0:T(8,128)S(1)} %copy-done.5, ...), custom_call_target="tpu_custom_call" | custom-call | tf_op jit(solution)/shard_map/gated_outputs/pallas_call | solution.py:354
  87.5 6.2 %convolution_convert_fusion.3 = bf16[256,2048]{1,0:T(8,128)(2,1)S(1)} fusion(bf16[2048,2048]{1,0:T(8,128)(2,1)} %param.29, bf16[512,2048]{1,0:T(8,128)(2,1)} %get-tuple-element.16), kind=kOutput, calls=%fused_computation.6 | convolution fusion | flops 2148007936 | bytes 10485760 | tf_op jit(solution)/shard_map/dot_general | solution.py:424
  93.7 1.5 collective-permute-start.1
  95.2 23.8 %collective-permute-done.1 = bf16[256,2048]{1,0:T(8,128)(2,1)S(1)} collective-permute-done((bf16[256,2048]{1,0:T(8,128)(2,1)S(1)}, bf16[256,2048]{1,0:T(8,128)(2,1)S(1)}, u32[]{:S(2)}, u32[]{:S(2)}) %collective-permute-start.1) | collective-permute-done | bytes 1048608 | tf_op jit(solution)/shard_map/ppermute | solution.py:418
  119.0 3.6 %convert_add_fusion = f32[256,2048]{1,0:T(8,128)S(1)} fusion(bf16[256,2048]{1,0:T(8,128)(2,1)S(1)} %collective-permute-done.1, bf16[2048,2048]{1,0:T(8,128)(2,1)S(1)} %bitcast.39, bf16[512,2048]{1,0:T(8,128)(2,1)} %get-tuple-element.16), kind=kOutput, calls=%fused_computation.7 | convolution fusion | flops 2148532224 | bytes 12582912 | tf_op jit(solution)/shard_map/dot_general | solution.py:425
  122.7 1.6 collective-permute-start.2
  124.2 0.6 collective-permute-start.8
  124.8 11.2 %collective-permute-done.2 = bf16[128,2048]{1,0:T(8,128)(2,1)S(1)} collective-permute-done((bf16[128,2048]{1,0:T(8,128)(2,1)S(1)}, bf16[128,2048]{1,0:T(8,128)(2,1)S(1)}, u32[]{:S(2)}, u32[]{:S(2)}) %collective-permute-start.2) | collective-permute-done | bytes 524320 | tf_op jit(solution)/shard_map/ppermute | solution.py:418
  136.0 0.1 slice_add_fusion.3
  136.2 2.5 collective-permute-start.3
  138.6 7.0 %convolution_convert_fusion.2 = bf16[256,2048]{1,0:T(8,128)(2,1)} fusion(bf16[2048,2048]{1,0:T(8,128)(2,1)} %collective-permute-done.4, bf16[512,2048]{1,0:T(8,128)(2,1)} %get-tuple-element.16), kind=kOutput, calls=%fused_computation.5 | convolution fusion | flops 2148007936 | bytes 10485760 | tf_op jit(solution)/shard_map/dot_general | solution.py:424
  145.6 1.5 collective-permute-start.5
  147.1 2.4 collective-permute-done.3
  149.6 0.4 copy.20
  150.0 0.5 broadcast_in_dim.37
  150.5 3.5 %dynamic_update_slice.12 = bf16[64,4,2048]{2,1,0:T(4,128)(2,1)S(1)} dynamic-update-slice(bf16[64,4,2048]{2,1,0:T(4,128)(2,1)S(1)} %broadcast_in_dim.37, bf16[64,1,2048]{2,1,0:T(2,128)(2,1)S(1)} %copy.20, s32[]{:T(128)} %constant.61.clone.1, s32[]{:T(128)S(6)} %select_n.59, s32[]{:T(128)} %constant.61.clone.1) | dynamic-update-slice | bytes 524292 | tf_op jit(solution)/shard_map/dynamic_update_slice | solution.py:441
  154.0 17.2 %collective-permute-done.8 = bf16[512,2048]{1,0:T(8,128)(2,1)} collective-permute-done((bf16[512,2048]{1,0:T(8,128)(2,1)}, bf16[512,2048]{1,0:T(8,128)(2,1)}, u32[]{:S(2)}, u32[]{:S(2)}) %collective-permute-start.8) | collective-permute-done | bytes 2097184 | tf_op jit(solution)/shard_map/ppermute | solution.py:413
  171.2 6.2 %convolution_convert_fusion.1 = bf16[256,2048]{1,0:T(8,128)(2,1)S(1)} fusion(bf16[2048,2048]{1,0:T(8,128)(2,1)} %param.29, bf16[512,2048]{1,0:T(8,128)(2,1)} %collective-permute-done.8), kind=kOutput, calls=%fused_computation.4 | convolution fusion | flops 2148007936 | bytes 10485760 | tf_op jit(solution)/shard_map/dot_general | solution.py:424
  177.4 1.5 collective-permute-start.9
  179.0 6.0 %convolution_convert_fusion = bf16[256,2048]{1,0:T(8,128)(2,1)S(1)} fusion(bf16[2048,2048]{1,0:T(8,128)(2,1)} %collective-permute-done.4, bf16[512,2048]{1,0:T(8,128)(2,1)} %collective-permute-done.8), kind=kOutput, calls=%fused_computation.3 | convolution fusion | flops 2148007936 | bytes 10485760 | tf_op jit(solution)/shard_map/dot_general | solution.py:424
  185.0 0.9 collective-permute-start.13
  185.9 6.1 %convolution_add_fusion.2 = f32[256,2048]{1,0:T(8,128)S(1)} fusion(bf16[2048,2048]{1,0:T(8,128)(2,1)} %collective-permute-done.4, bf16[256,2048]{1,0:T(8,128)(2,1)S(1)} %collective-permute-done.5, bf16[512,2048]{1,0:T(8,128)(2,1)} %get-tuple-element.16), kind=kOutput, calls=%fused_computation.2 | convolution fusion | flops 2148532224 | bytes 12582912 | tf_op jit(solution)/shard_map/dot_general | solution.py:425
  192.1 0.6 collective-permute-start.6
  192.7 10.9 %collective-permute-done.9 = bf16[256,2048]{1,0:T(8,128)(2,1)S(1)} collective-permute-done((bf16[256,2048]{1,0:T(8,128)(2,1)S(1)}, bf16[256,2048]{1,0:T(8,128)(2,1)S(1)}, u32[]{:S(2)}, u32[]{:S(2)}) %collective-permute-start.9) | collective-permute-done | bytes 1048608 | tf_op jit(solution)/shard_map/ppermute | solution.py:418
  203.6 3.7 %convolution_add_fusion.1 = f32[256,2048]{1,0:T(8,128)S(1)} fusion(bf16[2048,2048]{1,0:T(8,128)(2,1)S(1)} %bitcast.41, bf16[256,2048]{1,0:T(8,128)(2,1)S(1)} %collective-permute-done.9, bf16[512,2048]{1,0:T(8,128)(2,1)} %collective-permute-done.8), kind=kOutput, calls=%fused_computation.1 | convolution fusion | flops 2148532224 | bytes 12582912 | tf_op jit(solution)/shard_map/dot_general | solution.py:425
  207.3 0.6 collective-permute-start.10
  207.9 15.3 %collective-permute-done.13 = bf16[256,2048]{1,0:T(8,128)(2,1)S(1)} collective-permute-done((bf16[256,2048]{1,0:T(8,128)(2,1)S(1)}, bf16[256,2048]{1,0:T(8,128)(2,1)S(1)}, u32[]{:S(2)}, u32[]{:S(2)}) %collective-permute-start.13) | collective-permute-done | bytes 1048608 | tf_op jit(solution)/shard_map/ppermute | solution.py:418
  223.3 6.1 %convolution_add_fusion = f32[256,2048]{1,0:T(8,128)S(1)} fusion(bf16[2048,2048]{1,0:T(8,128)(2,1)} %collective-permute-done.4, bf16[256,2048]{1,0:T(8,128)(2,1)S(1)} %collective-permute-done.13, bf16[512,2048]{1,0:T(8,128)(2,1)} %collective-permute-done.8), kind=kOutput, calls=%fused_computation | convolution fusion | flops 2148532224 | bytes 12582912 | tf_op jit(solution)/shard_map/dot_general | solution.py:425
  229.4 0.6 collective-permute-start.14
  230.0 0.1 slice_add_fusion.2
  230.2 2.5 collective-permute-start.7
  232.6 0.1 slice_add_fusion.1
  232.8 0.6 collective-permute-start.11
  233.4 18.5 %collective-permute-done.14 = bf16[128,2048]{1,0:T(8,128)(2,1)S(1)} collective-permute-done((bf16[128,2048]{1,0:T(8,128)(2,1)S(1)}, bf16[128,2048]{1,0:T(8,128)(2,1)S(1)}, u32[]{:S(2)}, u32[]{:S(2)}) %collective-permute-start.14) | collective-permute-done | bytes 524320 | tf_op jit(solution)/shard_map/ppermute | solution.py:418
  251.9 0.1 slice_add_fusion
  252.2 0.6 collective-permute-start.12
  252.8 12.1 %collective-permute-done.15 = bf16[64,2048]{1,0:T(8,128)(2,1)S(1)} collective-permute-done((bf16[64,2048]{1,0:T(8,128)(2,1)S(1)}, bf16[64,2048]{1,0:T(8,128)(2,1)S(1)}, u32[]{:S(2)}, u32[]{:S(2)}) %collective-permute-start.15) | collective-permute-done | bytes 262176 | tf_op jit(solution)/shard_map/ppermute | solution.py:418
  265.0 0.6 collective-permute-start.16
  265.7 0.4 copy.21
  266.1 3.3 %dynamic_update_slice.13 = bf16[64,4,2048]{2,1,0:T(4,128)(2,1)S(1)} dynamic-update-slice(bf16[64,4,2048]{2,1,0:T(4,128)(2,1)S(1)} %dynamic_update_slice.12, bf16[64,1,2048]{2,1,0:T(2,128)(2,1)S(1)} %copy.21, s32[]{:T(128)} %constant.61.clone.1, s32[]{:T(128)S(6)} %select_n.60, s32[]{:T(128)} %constant.61.clone.1) | dynamic-update-slice | bytes 524292 | tf_op jit(solution)/shard_map/dynamic_update_slice | solution.py:444
  269.4 0.4 copy.22
  269.8 3.5 %collective-permute-done.16 = bf16[64,2048]{1,0:T(8,128)(2,1)S(1)} collective-permute-done((bf16[64,2048]{1,0:T(8,128)(2,1)S(1)}, bf16[64,2048]{1,0:T(8,128)(2,1)S(1)}, u32[]{:S(2)}, u32[]{:S(2)}) %collective-permute-start.16) | collective-permute-done | bytes 262176 | tf_op jit(solution)/shard_map/ppermute | solution.py:413
  273.3 0.4 copy.23
  273.7 3.3 %dynamic_update_slice.14 = bf16[64,4,2048]{2,1,0:T(4,128)(2,1)S(1)} dynamic-update-slice(bf16[64,4,2048]{2,1,0:T(4,128)(2,1)S(1)} %dynamic_update_slice.13, bf16[64,1,2048]{2,1,0:T(2,128)(2,1)S(1)} %copy.22, s32[]{:T(128)} %constant.61.clone.1, s32[]{:T(128)S(6)} %select_n.62, s32[]{:T(128)} %constant.61.clone.1) | dynamic-update-slice | bytes 524292 | tf_op jit(solution)/shard_map/dynamic_update_slice | solution.py:441
  277.0 3.3 %dynamic_update_slice.15 = bf16[64,4,2048]{2,1,0:T(4,128)(2,1)S(1)} dynamic-update-slice(bf16[64,4,2048]{2,1,0:T(4,128)(2,1)S(1)} %dynamic_update_slice.14, bf16[64,1,2048]{2,1,0:T(2,128)(2,1)S(1)} %copy.23, s32[]{:T(128)} %constant.61.clone.1, s32[]{:T(128)S(6)} %select_n.63, s32[]{:T(128)} %constant.61.clone.1) | dynamic-update-slice | bytes 524292 | tf_op jit(solution)/shard_map/dynamic_update_slice | solution.py:444
  280.2 1.6 copy.24
  (54 shorter events, 0.9 us)
Async XLA Ops:
  7.2 65.4 %all-gather.3.cloned.1.call-start = ((), (), s32[]{:S(2)}) async-start(), calls=%async_computation | async-start | bytes 5570560 | tf_op jit(solution)/shard_map/all_gather | solution.py:324
  8.9 3.8 %collective-permute-start = (bf16[3,2560]{1,0:T(4,128)(2,1)S(1)}, bf16[3,2560]{1,0:T(4,128)(2,1)S(1)}, u32[]{:S(2)}, u32[]{:S(2)}) collective-permute-start(bf16[3,2560]{1,0:T(4,128)(2,1)S(1)} %pad_maximum_fusion), channel_id=1, source_target_pairs={{0,8},{8,16},{16,24},{1,9},{9,17},{17,25},{2,10},{10,18},{18,26},{... | collective-permute-start | bytes 46088 | tf_op jit(solution)/shard_map/ppermute | solution.py:257
  13.5 0.8 copy-start.4
  14.3 0.8 copy-start.6
  15.2 0.7 copy-start.7
  15.9 0.8 copy-start.8
  16.7 0.7 copy-start.10
  17.4 17.9 %copy-start.5 = (f32[32,512]{1,0:T(8,128)S(1)}, f32[32,512]{1,0:T(8,128)}, u32[]{:S(2)}) copy-start(f32[32,512]{1,0:T(8,128)} %dt.5) | copy-start | bytes 196612
  17.4 17.9 %copy-start.11 = (f32[32]{0:T(128)S(1)}, f32[32]{0:T(128)}, u32[]{:S(2)}) copy-start(f32[32]{0:T(128)} %param.20) | copy-start | bytes 388
  29.8 1.3 copy-start.1
  31.1 1.3 copy-start.2
  32.5 106.2 %collective-permute-start.4 = (bf16[2048,2048]{1,0:T(8,128)(2,1)}, bf16[2048,2048]{1,0:T(8,128)(2,1)}, u32[]{:S(2)}, u32[]{:S(2)}) collective-permute-start(bf16[2048,2048]{1,0:T(8,128)(2,1)} %param.29), channel_id=1, source_target_pairs={{0,8},{8,0},{16,24},{24,16},{1,9},{9,1},{17,25},{25,17},{2,10},{10... | collective-permute-start | bytes 25165832 | tf_op jit(solution)/shard_map/ppermute | solution.py:246
  35.2 1.6 copy-start.3
  36.8 35.8 %copy-start = (bf16[512,2048]{1,0:T(8,128)(2,1)S(1)}, bf16[512,2048]{1,0:T(8,128)(2,1)}, u32[]{:S(2)}) copy-start(bf16[512,2048]{1,0:T(8,128)(2,1)} %gate.1) | copy-start | bytes 6291460
  36.8 35.8 %copy-start.9 = (f32[2048]{0:T(1024)S(1)}, f32[2048]{0:T(1024)}, u32[]{:S(2)}) copy-start(f32[2048]{0:T(1024)} %param.28) | copy-start | bytes 24580
  72.6 46.4 %slice-start = ((s8[8388608]{0:T(1024)(128)(4,1)}), s8[4194304]{0:T(1024)(128)(4,1)S(1)}, s32[]{:S(2)}) async-start(s8[8388608]{0:T(1024)(128)(4,1)} %bitcast.38), calls=%async_computation.1 | async-start | bytes 8388608
  87.5 31.6 %slice-start.1 = ((s8[8388608]{0:T(1024)(128)(4,1)}), s8[4194304]{0:T(1024)(128)(4,1)S(1)}, s32[]{:S(2)}) async-start(s8[8388608]{0:T(1024)(128)(4,1)} %bitcast.38), calls=%async_computation.2 | async-start | bytes 8388608
  93.7 25.4 %collective-permute-start.1 = (bf16[256,2048]{1,0:T(8,128)(2,1)S(1)}, bf16[256,2048]{1,0:T(8,128)(2,1)S(1)}, u32[]{:S(2)}, u32[]{:S(2)}) collective-permute-start(bf16[256,2048]{1,0:T(8,128)(2,1)S(1)} %convolution_convert_fusion.3), channel_id=1, source_target_pairs={{0,1},{1,0},{2,3},{3,2},{4,5},{5,4},{6,7},{7,6},{8,9},{9,8},{10,11... | collective-permute-start | bytes 3145736 | tf_op jit(solution)/shard_map/ppermute | solution.py:418
  122.7 13.3 %collective-permute-start.2 = (bf16[128,2048]{1,0:T(8,128)(2,1)S(1)}, bf16[128,2048]{1,0:T(8,128)(2,1)S(1)}, u32[]{:S(2)}, u32[]{:S(2)}) collective-permute-start(bf16[128,2048]{1,0:T(8,128)(2,1)S(1)} %slice.167), channel_id=1, source_target_pairs={{0,2},{1,3},{2,0},{3,1},{4,6},{5,7},{6,4},{7,5},{8,10},{9,11},{10,... | collective-permute-start | bytes 1572872 | tf_op jit(solution)/shard_map/ppermute | solution.py:418
  124.2 47.0 %collective-permute-start.8 = (bf16[512,2048]{1,0:T(8,128)(2,1)}, bf16[512,2048]{1,0:T(8,128)(2,1)}, u32[]{:S(2)}, u32[]{:S(2)}) collective-permute-start(bf16[512,2048]{1,0:T(8,128)(2,1)} %get-tuple-element.16), channel_id=1, source_target_pairs={{0,16},{8,24},{16,0},{24,8},{1,17},{9,25},{17,1},{25,9},{2,18},{10... | collective-permute-start | bytes 6291464 | tf_op jit(solution)/shard_map/ppermute | solution.py:413
  136.2 13.4 %collective-permute-start.3 = (bf16[64,2048]{1,0:T(8,128)(2,1)S(1)}, bf16[64,2048]{1,0:T(8,128)(2,1)S(1)}, u32[]{:S(2)}, u32[]{:S(2)}) collective-permute-start(bf16[64,2048]{1,0:T(8,128)(2,1)S(1)} %slice.171), channel_id=1, source_target_pairs={{0,4},{1,5},{2,6},{3,7},{4,0},{5,1},{6,2},{7,3},{8,12},{9,13},{10,... | collective-permute-start | bytes 786440 | tf_op jit(solution)/shard_map/ppermute | solution.py:418
  145.6 40.3 %collective-permute-start.5 = (bf16[256,2048]{1,0:T(8,128)(2,1)}, bf16[256,2048]{1,0:T(8,128)(2,1)S(1)}, u32[]{:S(2)}, u32[]{:S(2)}) collective-permute-start(bf16[256,2048]{1,0:T(8,128)(2,1)} %convolution_convert_fusion.2), channel_id=1, source_target_pairs={{0,1},{1,0},{2,3},{3,2},{4,5},{5,4},{6,7},{7,6},{8,9},{9,8},{10,11... | collective-permute-start | bytes 3145736 | tf_op jit(solution)/shard_map/ppermute | solution.py:418
  171.2 32.4 %slice-start.2 = ((s8[8388608]{0:T(1024)(128)(4,1)}), s8[4194304]{0:T(1024)(128)(4,1)S(1)}, s32[]{:S(2)}) async-start(s8[8388608]{0:T(1024)(128)(4,1)} %bitcast.40), calls=%async_computation.3 | async-start | bytes 8388608
  177.4 26.2 %slice-start.3 = ((s8[8388608]{0:T(1024)(128)(4,1)}), s8[4194304]{0:T(1024)(128)(4,1)S(1)}, s32[]{:S(2)}) async-start(s8[8388608]{0:T(1024)(128)(4,1)} %bitcast.40), calls=%async_computation.4 | async-start | bytes 8388608
  177.4 26.2 %collective-permute-start.9 = (bf16[256,2048]{1,0:T(8,128)(2,1)S(1)}, bf16[256,2048]{1,0:T(8,128)(2,1)S(1)}, u32[]{:S(2)}, u32[]{:S(2)}) collective-permute-start(bf16[256,2048]{1,0:T(8,128)(2,1)S(1)} %convolution_convert_fusion.1), channel_id=1, source_target_pairs={{0,1},{1,0},{2,3},{3,2},{4,5},{5,4},{6,7},{7,6},{8,9},{9,8},{10,11... | collective-permute-start | bytes 3145736 | tf_op jit(solution)/shard_map/ppermute | solution.py:418
  185.0 38.2 %collective-permute-start.13 = (bf16[256,2048]{1,0:T(8,128)(2,1)S(1)}, bf16[256,2048]{1,0:T(8,128)(2,1)S(1)}, u32[]{:S(2)}, u32[]{:S(2)}) collective-permute-start(bf16[256,2048]{1,0:T(8,128)(2,1)S(1)} %convolution_convert_fusion), channel_id=1, source_target_pairs={{0,1},{1,0},{2,3},{3,2},{4,5},{5,4},{6,7},{7,6},{8,9},{9,8},{10,11... | collective-permute-start | bytes 3145736 | tf_op jit(solution)/shard_map/ppermute | solution.py:418
  192.1 38.0 %collective-permute-start.6 = (bf16[128,2048]{1,0:T(8,128)(2,1)S(1)}, bf16[128,2048]{1,0:T(8,128)(2,1)S(1)}, u32[]{:S(2)}, u32[]{:S(2)}) collective-permute-start(bf16[128,2048]{1,0:T(8,128)(2,1)S(1)} %slice.166), channel_id=1, source_target_pairs={{0,2},{1,3},{2,0},{3,1},{4,6},{5,7},{6,4},{7,5},{8,10},{9,11},{10,... | collective-permute-start | bytes 1572872 | tf_op jit(solution)/shard_map/ppermute | solution.py:418
  207.3 25.3 %collective-permute-start.10 = (bf16[128,2048]{1,0:T(8,128)(2,1)S(1)}, bf16[128,2048]{1,0:T(8,128)(2,1)S(1)}, u32[]{:S(2)}, u32[]{:S(2)}) collective-permute-start(bf16[128,2048]{1,0:T(8,128)(2,1)S(1)} %slice.165), channel_id=1, source_target_pairs={{0,2},{1,3},{2,0},{3,1},{4,6},{5,7},{6,4},{7,5},{8,10},{9,11},{10,... | collective-permute-start | bytes 1572872 | tf_op jit(solution)/shard_map/ppermute | solution.py:418
  229.4 22.4 %collective-permute-start.14 = (bf16[128,2048]{1,0:T(8,128)(2,1)S(1)}, bf16[128,2048]{1,0:T(8,128)(2,1)S(1)}, u32[]{:S(2)}, u32[]{:S(2)}) collective-permute-start(bf16[128,2048]{1,0:T(8,128)(2,1)S(1)} %slice.164), channel_id=1, source_target_pairs={{0,2},{1,3},{2,0},{3,1},{4,6},{5,7},{6,4},{7,5},{8,10},{9,11},{10,... | collective-permute-start | bytes 1572872 | tf_op jit(solution)/shard_map/ppermute | solution.py:418
  230.2 35.4 %collective-permute-start.7 = (bf16[64,2048]{1,0:T(8,128)(2,1)S(1)}, bf16[64,2048]{1,0:T(8,128)(2,1)S(1)}, u32[]{:S(2)}, u32[]{:S(2)}) collective-permute-start(bf16[64,2048]{1,0:T(8,128)(2,1)S(1)} %slice.170), channel_id=1, source_target_pairs={{0,4},{1,5},{2,6},{3,7},{4,0},{5,1},{6,2},{7,3},{8,12},{9,13},{10,... | collective-permute-start | bytes 786440 | tf_op jit(solution)/shard_map/ppermute | solution.py:418
  232.8 19.3 %collective-permute-start.11 = (bf16[64,2048]{1,0:T(8,128)(2,1)S(1)}, bf16[64,2048]{1,0:T(8,128)(2,1)S(1)}, u32[]{:S(2)}, u32[]{:S(2)}) collective-permute-start(bf16[64,2048]{1,0:T(8,128)(2,1)S(1)} %slice.169), channel_id=1, source_target_pairs={{0,4},{1,5},{2,6},{3,7},{4,0},{5,1},{6,2},{7,3},{8,12},{9,13},{10,... | collective-permute-start | bytes 786440 | tf_op jit(solution)/shard_map/ppermute | solution.py:418
  252.0 12.9 %collective-permute-start.15 = (bf16[64,2048]{1,0:T(8,128)(2,1)S(1)}, bf16[64,2048]{1,0:T(8,128)(2,1)S(1)}, u32[]{:S(2)}, u32[]{:S(2)}) collective-permute-start(bf16[64,2048]{1,0:T(8,128)(2,1)S(1)} %slice.168), channel_id=1, source_target_pairs={{0,4},{1,5},{2,6},{3,7},{4,0},{5,1},{6,2},{7,3},{8,12},{9,13},{10,... | collective-permute-start | bytes 786440 | tf_op jit(solution)/shard_map/ppermute | solution.py:418
  252.2 17.2 %collective-permute-start.12 = (bf16[64,2048]{1,0:T(8,128)(2,1)S(1)}, bf16[64,2048]{1,0:T(8,128)(2,1)S(1)}, u32[]{:S(2)}, u32[]{:S(2)}) collective-permute-start(bf16[64,2048]{1,0:T(8,128)(2,1)S(1)} %fusion.12), channel_id=1, source_target_pairs={{0,16},{8,24},{16,0},{24,8},{1,17},{9,25},{17,1},{25,9},{2,18},{10... | collective-permute-start | bytes 786440 | tf_op jit(solution)/shard_map/ppermute | solution.py:413
  265.0 8.3 %collective-permute-start.16 = (bf16[64,2048]{1,0:T(8,128)(2,1)S(1)}, bf16[64,2048]{1,0:T(8,128)(2,1)S(1)}, u32[]{:S(2)}, u32[]{:S(2)}) collective-permute-start(bf16[64,2048]{1,0:T(8,128)(2,1)S(1)} %fusion.11), channel_id=1, source_target_pairs={{0,16},{8,24},{16,0},{24,8},{1,17},{9,25},{17,1},{25,9},{2,18},{10... | collective-permute-start | bytes 786440 | tf_op jit(solution)/shard_map/ppermute | solution.py:413
Sparse Core Ops, SparseCore 0:
  32.6 39.9 all-gather.2

commit v2 on v1

--- a/solution.py
+++ b/solution.py
@@ -21,6 +21,7 @@
 norm_eps = 1e-05
 f32 = jnp.float32
 bf16 = jnp.bfloat16
+MESH = pl.DeviceIdType.MESH
 
 
 def silu(v):
@@ -207,6 +208,211 @@
         if whole_group:
             value = value * inverse[rows] * gain[...]
         normed_out[pl.ds(place, block), :] = value.astype(normed_out.dtype)
+
+
+def partner_of(place, bit):
+    size = 1 << bit
+    return place + (1 - 2 * ((place // size) % 2)) * size
+
+
+def project_kernel(
+    act, w_own, w_other, out,
+    w, act_x, keep, y_send, y_recv, a_send, a_recv, b_send, b_recv, x_send, x_recv,
+    w_sem, act_sem, send_sem, recv_sem, x_send_sem, x_recv_sem,
+):
+    seq = lax.axis_index("seq")
+    head = lax.axis_index("head")
+    wide = w.shape[2]
+    per = w_own.shape[1] // wide
+    half = 2 * per
+    count = 2 * half
+    block = out.shape[0]
+    other_chip = (seq + 2) % 4
+    across = [{"head": partner_of(head, bit)} for bit in range(3)]
+    over_x = {"seq": other_chip}
+
+    def load(k, source, first):
+        return pltpu.make_async_copy(
+            source.at[:, pl.ds(pl.multiple_of((k - first) * wide, wide), wide)],
+            w.at[k], w_sem.at[k],
+        )
+
+    def start_own(k, carry):
+        load(k, w_own, 0).start()
+        return carry
+
+    def start_other(k, carry):
+        load(k, w_other, per).start()
+        return carry
+
+    lax.fori_loop(0, per, start_own, 0)
+    lax.fori_loop(per, half, start_other, 0)
+
+    barrier = pltpu.get_barrier_semaphore()
+    for target in across + [over_x]:
+        pl.semaphore_signal(barrier, inc=1, device_id=target, device_id_type=MESH)
+    pl.semaphore_wait(barrier, 4)
+
+    def act_copy():
+        return pltpu.make_async_remote_copy(
+            src_ref=act, dst_ref=act_x, send_sem=act_sem.at[0], recv_sem=act_sem.at[1],
+            device_id=over_x, device_id_type=MESH,
+        )
+
+    def head_copy(stage, t):
+        source, target = ((y_send, y_recv), (a_send, a_recv), (b_send, b_recv))[stage]
+        return pltpu.make_async_remote_copy(
+            src_ref=source.at[t], dst_ref=target.at[t],
+            send_sem=send_sem.at[stage, t], recv_sem=recv_sem.at[stage, t],
+            device_id=across[stage], device_id_type=MESH,
+        )
+
+    def chip_copy(k):
+        return pltpu.make_async_remote_copy(
+            src_ref=x_send.at[k], dst_ref=x_recv.at[k],
+            send_sem=x_send_sem.at[k], recv_sem=x_recv_sem.at[k],
+            device_id=over_x, device_id_type=MESH,
+        )
+
+    act_copy().start()
+
+    def multiply(source, t, k):
+        y_send[t] = jnp.dot(
+            source[4 * block :], w[k], preferred_element_type=f32
+        ).astype(bf16)
+        head_copy(0, t).start()
+        keep[t] = jnp.dot(source[: 4 * block], w[k], preferred_element_type=f32)
+
+    def column(k, home):
+        core = home % 2
+        return ((home // 2) * 2 + (core + k // per) % 2) * (per * wide) + (k % per) * wide
+
+    def first_stage(t):
+        head_copy(0, t).wait_recv()
+        a_send[t] = (keep[t, 2 * block :] + y_recv[t, 2 * block :].astype(f32)).astype(bf16)
+        head_copy(1, t).start()
+        keep[t, : 2 * block] = keep[t, : 2 * block] + y_recv[t, : 2 * block].astype(f32)
+
+    def second_stage(t):
+        head_copy(1, t).wait_recv()
+        b_send[t] = (keep[t, block : 2 * block] + a_recv[t, block:].astype(f32)).astype(bf16)
+        head_copy(2, t).start()
+        keep[t, :block] = keep[t, :block] + a_recv[t, :block].astype(f32)
+
+    def third_stage(t):
+        head_copy(2, t).wait_recv()
+        return (keep[t, :block] + b_recv[t].astype(f32)).astype(bf16)
+
+    def finish_own(t):
+        out[:, pl.ds(pl.multiple_of(column(t, seq), wide), wide)] = third_stage(t)
+
+    def finish_far(t):
+        x_send[t - half] = third_stage(t)
+        chip_copy(t - half).start()
+
+    def stages(t):
+        first_stage(t)
+
+        @pl.when(t >= 1)
+        def _():
+            second_stage(t - 1)
+
+        @pl.when((t >= 2) & (t < half + 2))
+        def _():
+            finish_own(t - 2)
+
+        @pl.when(t >= half + 2)
+        def _():
+            finish_far(t - 2)
+
+    def begin(t, carry):
+        @pl.when(t < per)
+        def _():
+            load(t, w_own, 0).wait()
+
+        @pl.when(t >= per)
+        def _():
+            load(t, w_other, per).wait()
+
+        multiply(act, t, t)
+        return carry
+
+    ahead = 2
+
+    def only_stages(t, carry):
+        stages(t)
+        return carry
+
+    def both(t, carry):
+        multiply(act_x, t + ahead, t + ahead - half)
+        stages(t)
+        return carry
+
+    lax.fori_loop(0, half, begin, 0)
+    lax.fori_loop(0, half - ahead, only_stages, 0)
+    act_copy().wait_recv()
+    lax.fori_loop(half - ahead, count - ahead, both, 0)
+    lax.fori_loop(count - ahead, count, only_stages, 0)
+    second_stage(count - 1)
+    finish_far(count - 2)
+    finish_far(count - 1)
+
+    def collect(k, carry):
+        chip_copy(k).wait_recv()
+        out[:, pl.ds(pl.multiple_of(column(k, other_chip), wide), wide)] = x_recv[k]
+        chip_copy(k).wait_send()
+        return carry
+
+    def drain(t, carry):
+        for stage in range(3):
+            head_copy(stage, t).wait_send()
+        return carry
+
+    act_copy().wait_send()
+    lax.fori_loop(0, half, collect, 0)
+    lax.fori_loop(0, count, drain, 0)
+
+
+def project(normed, own, other):
+    rows, width = normed.shape
+    columns = own.shape[1]
+    block = rows // 8
+    wide = 512
+    half = 2 * columns // wide
+    count = 2 * half
+    return pl.pallas_call(
+        project_kernel,
+        in_specs=[
+            pl.BlockSpec(memory_space=pltpu.VMEM),
+            pl.BlockSpec(memory_space=pl.ANY),
+            pl.BlockSpec(memory_space=pl.ANY),
+        ],
+        out_specs=pl.BlockSpec(memory_space=pltpu.VMEM),
+        out_shape=jax.ShapeDtypeStruct((block, 4 * columns), bf16),
+        scratch_shapes=[
+            pltpu.VMEM((half, width, wide), bf16),
+            pltpu.VMEM((rows, width), bf16),
+            pltpu.VMEM((count, 4 * block, wide), f32),
+            pltpu.VMEM((count, 4 * block, wide), bf16),
+            pltpu.VMEM((count, 4 * block, wide), bf16),
+            pltpu.VMEM((count, 2 * block, wide), bf16),
+            pltpu.VMEM((count, 2 * block, wide), bf16),
+            pltpu.VMEM((count, block, wide), bf16),
+            pltpu.VMEM((count, block, wide), bf16),
+            pltpu.VMEM((half, block, wide), bf16),
+            pltpu.VMEM((half, block, wide), bf16),
+            pltpu.SemaphoreType.DMA((half,)),
+            pltpu.SemaphoreType.DMA((2,)),
+            pltpu.SemaphoreType.DMA((3, count)),
+            pltpu.SemaphoreType.DMA((3, count)),
+            pltpu.SemaphoreType.DMA((half,)),
+            pltpu.SemaphoreType.DMA((half,)),
+        ],
+        compiler_params=pltpu.CompilerParams(
+            vmem_limit_bytes=56 * 1024 * 1024, collective_id=0, has_side_effects=True
+        ),
+        name="project_and_sum",
+    )(normed, own, other)
 
 
 def params():
@@ -405,6 +611,9 @@
             (pieces * inverse[:, :, None]).reshape(rows, width) * norm_gain[None, :]
         ).astype(bf16)
 
+    if seq_count == 4 and head_count == 8 and whole_group and out_weight.shape[1] % 512 == 0:
+        return (project(normed, out_weight, other_core), boundary)
+
     chips = seq_count // 2
 
     def around(value, by):

time: 289 us -> 215 us (0.74)
  Pallas kernels: 37.7 us -> 148 us
  waiting for transfers between devices: 140 us -> 34 us
  matrix products: 44.8 us -> 0 us
  starting transfers between devices: 21.3 us -> 2.52 us
  local copies, waits for them, and re-layouts: 28.6 us -> 14.9 us
    ppermute x15 -> x0, waiting for transfers between devices: 115 us -> none  [the longest x12 94.3 us: across(): lax.ppermute(value, 'head', [(i, i ^ 1 << bit) for i in range(head_count)])]
    pallas_call x0 -> x1, Pallas kernels: none -> 111 us  [project(): pl.pallas_call(project_kernel, in_specs=[pl.BlockSpec(memory_space=pltpu....]
    dot_general x8 -> x0, matrix products: 44.8 us -> none  [the longest x4 25.4 us: reduced(): give = jnp.dot(act[half:], weight, preferred_element_type=f32).astype(bf16)]
    ppermute x15 -> x0, starting transfers between devices: 16.2 us -> none  [the longest x12 14.4 us: across(): lax.ppermute(value, 'head', [(i, i ^ 1 << bit) for i in range(head_count)])]
    dynamic_update_slice x4 -> x0, local copies, waits for them, and re-layouts: 13.3 us -> none  [the longest x2 6.76 us: body(): lax.dynamic_update_slice(layer_out, mine[:, None], (0, chip * 2 + core, 0))]
    ppermute x1, waiting for transfers between devices: 0.01 us -> 7.71 us  [body(): lax.ppermute(last_rows, 'seq', [(i, i + 1) for i in range(seq_count - 1)])]
    unnamed x33 -> x27, local copies, waits for them, and re-layouts: 9.72 us -> 11.8 us
  transfers between devices with their start and end apart: 18 -> 3, of which waited for: 10 -> 2; matrix products, arithmetic and copies ran while one was open for 19% -> 2% of each run, Pallas kernels for 9% -> 17%
where the time goes in v2:
time: 215 us; the launch traced here: 214 us
  Pallas kernels  148 us (69%)
  waiting for transfers between devices  34 us (16%)
  local copies, waits for them, and re-layouts  14.9 us (7%)
  between operations  14.1 us (7%)
  starting transfers between devices  2.52 us (1%)
    pallas_call x1, Pallas kernels, project(): pl.pallas_call(project_kernel, in_specs=[pl.BlockSpec(memory_space=pltpu....  111 us
    all_gather x1, waiting for transfers between devices, body(): gathered = lax.all_gather(sent, 'seq')  26.3 us
    pallas_call x1, Pallas kernels, body(): pl.pallas_call(functools.partial(output_kernel, block=block, whole_group=...  14 us
    pallas_call x1, Pallas kernels, body(): pl.pallas_call(state_kernel, grid_spec=pltpu.PrefetchScalarGridSpec(num_s...  12.3 us
    unnamed x27, local copies, waits for them, and re-layouts  11.8 us
    pallas_call x1, Pallas kernels, body(): pl.pallas_call(local_kernel, grid=(spans,), in_specs=[span_x, span_bc, sp...  10.4 us
    ppermute x1, waiting for transfers between devices, body(): lax.ppermute(last_rows, 'seq', [(i, i + 1) for i in range(seq_count - 1)])  7.71 us
  transfers between devices with their start and end apart: 3, of which 2 were waited for; matrix products, arithmetic and copies ran while one was open for 2% of the time, Pallas kernels for 17%

profile of v2, /device:TPU:0, one launch (start us, length us, event | category | flops | bytes accessed | tf_op | source)
XLA Modules:
  0.0 214.3 jit_solution(6900410845330705654)
XLA Ops:
  7.2 0.0 all-gather.3.cloned.1.call-start
  7.2 0.5 collective-permute-start.1
  7.7 0.9 slice.7
  8.6 0.8 slice.6
  9.4 2.0 collective-permute-start
  11.4 0.7 constant_dynamic-slice_fusion.3
  12.1 0.7 copy.17.rate
  12.8 7.7 %collective-permute-done = bf16[3,2560]{1,0:T(4,128)(2,1)S(1)} collective-permute-done((bf16[3,2560]{1,0:T(4,128)(2,1)S(1)}, bf16[3,2560]{1,0:T(4,128)(2,1)S(1)}, u32[]{:S(2)}, u32[]{:S(2)}) %collective-permute-start) | collective-permute-done | bytes 15392 | tf_op jit(solution)/shard_map/ppermute | solution.py:463
  20.5 0.7 maximum_select_fusion
  21.3 0.0 copy-start.5
  21.3 0.8 copy-done.5
  22.1 0.0 copy-start.7
  22.1 0.8 copy-done.7
  23.0 0.0 copy-start.8
  23.0 0.7 copy-done.8
  23.7 0.0 copy-start.9
  23.7 0.8 copy-done.9
  24.5 0.0 copy-start.11
  24.5 0.7 copy-done.11
  25.2 0.0 copy-start.6
  25.2 0.0 copy-start.12
  25.2 12.3 %conv_and_states.1 = (bf16[512,2048]{1,0:T(8,128)(2,1)S(1)}, bf16[512,256]{1,0:T(8,128)(2,1)S(1)}, bf16[512,256]{1,0:T(8,128)(2,1)S(1)}, bf16[4,256,2048]{2,1,0:...) custom-call(s32[1]{0:T(128)} %bitcast.1.g_ref, bf16[512,2048]{1,0:T(8,128)(2,1)} %inner.1, ...), custom_call_target="tpu_custom_call" | custom-call | tf_op jit(solution)/shard_map/conv_and_states/pallas_call | solution.py:476
  37.5 0.0 copy-start.1
  37.5 1.4 copy-done.1
  38.9 0.0 copy-start.3
  38.9 1.3 copy-done.3
  40.2 0.0 all-gather.3.cloned.1.call-update
  40.3 0.1 pad_add_fusion.meta
  40.3 0.0 copy-done.6
  40.3 0.0 copy-done.12
  40.3 0.0 copy-start.4
  40.3 1.6 copy-done.4
  41.9 0.0 copy-start
  41.9 0.0 copy-start.10
  41.9 10.4 %local_outputs.1.y = f32[512,2048]{1,0:T(8,128)} custom-call(bf16[512,2048]{1,0:T(8,128)(2,1)S(1)} %copy-done.4, bf16[512,256]{1,0:T(8,128)(2,1)S(1)} %get-tuple-element.11.b, bf16[512,256]{1,0:T(8,128)(2,1)S(1)} %get-tuple-element.12.c, f32[32,512]{1,0:T(8,128)S(1)} %copy-done.6, f32[32,1]{1,0:T(8,128)S(1)} %copy.17.rate, f32[1,32]{1,0:T(1,128)S(1)} %bitcast.14, ...), custom_call_target="tpu_custom_call" | custom-call | flops 1073741824 | bytes 8388608 | tf_op jit(solution)/shard_map/local_outputs/pallas_call | solution.py:532
  52.4 26.3 %all-gather.3.cloned.1.call-done = bf16[1088,2048]{1,0:T(8,128)(2,1)} async-done(((bf16[272,2048]{1,0:T(8,128)(2,1)}), bf16[1088,2048]{1,0:T(8,128)(2,1)}) %all-gather.3.cloned.1.call-update) | async-done | bytes 4456464 | tf_op jit(solution)/shard_map/all_gather | solution.py:530
  78.7 0.0 copy-done
  78.7 0.0 copy-done.10
  78.7 14.0 %gated_outputs.1 = (bf16[512,2048]{1,0:T(8,128)(2,1)S(1)}, f32[2048,256]{1,0:T(8,128)}) custom-call(s32[9]{0:T(128)S(1)} %pad_add_fusion.meta, f32[512,2048]{1,0:T(8,128)} %local_outputs.1.y, bf16[512,256]{1,0:T(8,128)(2,1)S(1)} %get-tuple-element.12.c, bf16[512,2048]{1,0:T(8,128)(2,1)S(1)} %copy-done, f32[32,512]{1,0:T(8,128)S(1)} %copy-done.6, ...), custom_call_target="tpu_custom_call" | custom-call | tf_op jit(solution)/shard_map/gated_outputs/pallas_call | solution.py:560
  92.6 0.0 copy-start.2
  92.7 1.4 copy-done.2
  94.0 0.0 collective-permute-done.1.w_other
  94.0 111.1 %project_and_sum.1 = bf16[64,8192]{1,0:T(8,128)(2,1)} custom-call(bf16[512,2048]{1,0:T(8,128)(2,1)} %copy-done.2, bf16[2048,2048]{1,0:T(8,128)(2,1)} %w_own.1, bf16[2048,2048]{1,0:T(8,128)(2,1)} %collective-permute-done.1.w_other), custom_call_target="tpu_custom_call" | custom-call | tf_op jit(solution)/shard_map/project_and_sum/pallas_call | solution.py:383
  205.2 2.3 %copy.21 = bf16[64,8192]{1,0:T(8,128)(2,1)} copy(bf16[64,8192]{1,0:T(8,128)(2,1)} %project_and_sum.1) | data formatting | bytes 2097152
  (4 shorter events, 0.1 us)
Async XLA Ops:
  7.2 71.5 %all-gather.3.cloned.1.call-start = ((), (), s32[]{:S(2)}) async-start(), calls=%async_computation | async-start | bytes 5570560 | tf_op jit(solution)/shard_map/all_gather | solution.py:530
  7.2 86.8 %collective-permute-start.1 = (bf16[2048,2048]{1,0:T(8,128)(2,1)}, bf16[2048,2048]{1,0:T(8,128)(2,1)}, u32[]{:S(2)}, u32[]{:S(2)}) collective-permute-start(bf16[2048,2048]{1,0:T(8,128)(2,1)} %w_own.1), channel_id=1, source_target_pairs={{0,8},{8,0},{16,24},{24,16},{1,9},{9,1},{17,25},{25,17},{2,10},{10... | collective-permute-start | bytes 25165832 | tf_op jit(solution)/shard_map/ppermute | solution.py:452
  9.4 11.1 %collective-permute-start = (bf16[3,2560]{1,0:T(4,128)(2,1)S(1)}, bf16[3,2560]{1,0:T(4,128)(2,1)S(1)}, u32[]{:S(2)}, u32[]{:S(2)}) collective-permute-start(bf16[3,2560]{1,0:T(4,128)(2,1)S(1)} %pad_maximum_fusion), channel_id=1, source_target_pairs={{0,8},{8,16},{16,24},{1,9},{9,17},{17,25},{2,10},{10,18},{18,26},{... | collective-permute-start | bytes 46088 | tf_op jit(solution)/shard_map/ppermute | solution.py:463
  21.3 0.8 copy-start.5
  22.1 0.8 copy-start.7
  23.0 0.7 copy-start.8
  23.7 0.8 copy-start.9
  24.5 0.7 copy-start.11
  25.2 15.2 %copy-start.6 = (f32[32,512]{1,0:T(8,128)S(1)}, f32[32,512]{1,0:T(8,128)}, u32[]{:S(2)}) copy-start(f32[32,512]{1,0:T(8,128)} %dt.5) | copy-start | bytes 196612
  25.2 15.2 %copy-start.12 = (f32[32]{0:T(128)S(1)}, f32[32]{0:T(128)}, u32[]{:S(2)}) copy-start(f32[32]{0:T(128)} %param.20) | copy-start | bytes 388
  37.5 1.4 copy-start.1
  38.9 1.3 copy-start.3
  40.3 1.6 copy-start.4
  41.9 36.7 %copy-start = (bf16[512,2048]{1,0:T(8,128)(2,1)S(1)}, bf16[512,2048]{1,0:T(8,128)(2,1)}, u32[]{:S(2)}) copy-start(bf16[512,2048]{1,0:T(8,128)(2,1)} %gate.1) | copy-start | bytes 6291460
  41.9 36.7 %copy-start.10 = (f32[2048]{0:T(1024)S(1)}, f32[2048]{0:T(1024)}, u32[]{:S(2)}) copy-start(f32[2048]{0:T(1024)} %param.28) | copy-start | bytes 24580
  92.6 1.4 copy-start.2
Sparse Core Ops, SparseCore 0:
  40.4 38.2 all-gather.2

commit v3 on v2

--- a/solution.py
+++ b/solution.py
@@ -126,6 +126,91 @@
         high = tl.astype(bf16).astype(f32)
         row = lax.broadcasted_iota(jnp.int32, (EXTRA, tl.shape[1]), 0)
         send_out[STATE:] = jnp.where(row == 0, high, jnp.where(row == 1, tl - high, 0.0)).astype(bf16)
+
+
+PARTS = 4
+
+
+def chain_kernel(
+    x, b, c, dt, rate, skip, enter, local, sent, y_out, prior_out,
+    land, hop, send_sem, recv_sem,
+):
+    i = pl.program_id(0)
+    seq = lax.axis_index("seq")
+    last = 3
+    wide = land.shape[2]
+
+    def copy(k):
+        return pltpu.make_async_remote_copy(
+            src_ref=hop.at[k], dst_ref=land.at[k],
+            send_sem=send_sem.at[k], recv_sem=recv_sem.at[k],
+            device_id={"seq": (seq + 1) % 4}, device_id_type=MESH,
+        )
+
+    def joined(k):
+        cols = slice(k * wide, (k + 1) * wide)
+        own = sent[STATE : STATE + 1, cols].astype(f32) + sent[STATE + 1 : STATE + 2, cols].astype(f32)
+        tail = land[k, STATE:].astype(f32)
+        hop[k, :STATE] = (
+            jnp.exp(own) * land[k, :STATE].astype(f32) + local[:, cols]
+        ).astype(bf16)
+        log = tail[0:1] + tail[1:2] + own
+        high = log.astype(bf16).astype(f32)
+        row = lax.broadcasted_iota(jnp.int32, (EXTRA, wide), 0)
+        hop[k, STATE:] = jnp.where(row == 0, high, jnp.where(row == 1, log - high, 0.0)).astype(bf16)
+
+    @pl.when(i == 0)
+    def _():
+        barrier = pltpu.get_barrier_semaphore()
+
+        for by in (1, 3):
+            pl.semaphore_signal(
+                barrier, inc=1, device_id={"seq": (seq + by) % 4}, device_id_type=MESH
+            )
+        pl.semaphore_wait(barrier, 2)
+
+        @pl.when(seq == 0)
+        def _():
+            for k in range(PARTS):
+                hop[k] = sent[:, k * wide : (k + 1) * wide]
+                copy(k).start()
+
+        @pl.when(seq == 1)
+        def _():
+            for k in range(PARTS):
+                copy(k).wait_recv()
+                joined(k)
+                copy(k).start()
+
+    local_kernel(x, b, c, dt, rate, skip, enter, y_out)
+
+    @pl.when(i == pl.num_programs(0) - 1)
+    def _():
+        @pl.when(seq == 2)
+        def _():
+            for k in range(PARTS):
+                copy(k).wait_recv()
+                joined(k)
+                copy(k).start()
+
+        @pl.when(seq == 3)
+        def _():
+            for k in range(PARTS):
+                copy(k).wait_recv()
+
+        @pl.when(seq > 0)
+        def _():
+            for k in range(PARTS):
+                prior_out[:, k * wide : (k + 1) * wide] = land[k]
+
+        @pl.when(seq == 0)
+        def _():
+            prior_out[...] = jnp.zeros_like(prior_out)
+
+        @pl.when(seq < last)
+        def _():
+            for k in range(PARTS):
+                copy(k).wait_send()
 
 
 def local_kernel(x, b, c, dt, rate, skip, enter, y_out):
@@ -160,8 +245,8 @@
 
 
 def output_kernel(
-    meta, y, c, gate, dt, rate, gain, gathered, init, local, normed_out, boundary_out,
-    incoming, entering, mixed, offset, *, block, whole_group,
+    meta, y, c, gate, dt, rate, gain, gathered, own_tail, init, local, normed_out, boundary_out,
+    incoming, entering, mixed, offset, *, block, whole_group, chained,
 ):
     i = pl.program_id(0)
     heads = dt.shape[0]
@@ -173,13 +258,17 @@
         place = meta[0]
         rate_sum = jnp.zeros((1, width), f32)
         incoming[...] = jnp.zeros_like(incoming)
-        for k in range(count - 2, -1, -1):
+        if chained:
+            tail = gathered[0, STATE:].astype(f32)
+            incoming[...] = gathered[0, :STATE].astype(f32)
+            rate_sum = tail[0:1] + tail[1:2]
+        for k in range(-1 if chained else count - 2, -1, -1):
             live = k < place
             tail = gathered[k, STATE:].astype(f32)
             factor = jnp.where(live, jnp.exp(rate_sum), 0.0)
             incoming[...] += factor * gathered[k, :STATE].astype(f32)
             rate_sum = rate_sum + jnp.where(live, tail[0:1] + tail[1:2], 0.0)
-        tail = gathered[place, STATE:].astype(f32)
+        tail = (own_tail[...] if chained else gathered[place, STATE:]).astype(f32)
         own = jnp.exp(tail[0:1] + tail[1:2])
         for k in range(0, width, 256):
             cols = slice(k, k + 256)
@@ -217,7 +306,7 @@
 
 def project_kernel(
     act, w_own, w_other, out,
-    w, act_x, keep, y_send, y_recv, a_send, a_recv, b_send, b_recv, x_send, x_recv,
+    w, acts, act_x, keep, y_send, y_recv, a_send, a_recv, b_send, b_recv, x_send, x_recv,
     w_sem, act_sem, send_sem, recv_sem, x_send_sem, x_recv_sem,
 ):
     seq = lax.axis_index("seq")
@@ -228,7 +317,23 @@
     count = 2 * half
     block = out.shape[0]
     other_chip = (seq + 2) % 4
-    across = [{"head": partner_of(head, bit)} for bit in range(3)]
+    near = [partner_of(head, bit) for bit in range(3)]
+    across = [{"head": place} for place in near]
+
+    def turned(t):
+        return (t % 4) // 3
+
+    def target_of(stage, t):
+        if stage == 2:
+            return across[2]
+        return {"head": near[stage] + turned(t) * (near[1 - stage] - near[stage])}
+
+    def reorder(source, dest):
+        for part, first in enumerate((0, 4, 2, 6)):
+            dest[part * 2 * block : (part + 1) * 2 * block] = source[
+                first * block : (first + 2) * block
+            ]
+
     over_x = {"seq": other_chip}
 
     def load(k, source, first):
@@ -255,7 +360,7 @@
 
     def act_copy():
         return pltpu.make_async_remote_copy(
-            src_ref=act, dst_ref=act_x, send_sem=act_sem.at[0], recv_sem=act_sem.at[1],
+            src_ref=act, dst_ref=act_x.at[0], send_sem=act_sem.at[0], recv_sem=act_sem.at[1],
             device_id=over_x, device_id_type=MESH,
         )
 
@@ -264,7 +369,7 @@
         return pltpu.make_async_remote_copy(
             src_ref=source.at[t], dst_ref=target.at[t],
             send_sem=send_sem.at[stage, t], recv_sem=recv_sem.at[stage, t],
-            device_id=across[stage], device_id_type=MESH,
+            device_id=target_of(stage, t), device_id_type=MESH,
         )
 
     def chip_copy(k):
@@ -275,13 +380,16 @@
         )
 
     act_copy().start()
+    acts[0] = act[...]
+    reorder(act, acts.at[1])
 
     def multiply(source, t, k):
+        slot = turned(t)
         y_send[t] = jnp.dot(
-            source[4 * block :], w[k], preferred_element_type=f32
+            source[slot, 4 * block :], w[k], preferred_element_type=f32
         ).astype(bf16)
         head_copy(0, t).start()
-        keep[t] = jnp.dot(source[: 4 * block], w[k], preferred_element_type=f32)
+        keep[t] = jnp.dot(source[slot, : 4 * block], w[k], preferred_element_type=f32)
 
     def column(k, home):
         core = home % 2
@@ -334,7 +442,7 @@
         def _():
             load(t, w_other, per).wait()
 
-        multiply(act, t, t)
+        multiply(acts, t, t)
         return carry
 
     ahead = 2
@@ -351,6 +459,7 @@
     lax.fori_loop(0, half, begin, 0)
     lax.fori_loop(0, half - ahead, only_stages, 0)
     act_copy().wait_recv()
+    reorder(act_x.at[0], act_x.at[1])
     lax.fori_loop(half - ahead, count - ahead, both, 0)
     lax.fori_loop(count - ahead, count, only_stages, 0)
     second_stage(count - 1)
@@ -391,7 +500,8 @@
         out_shape=jax.ShapeDtypeStruct((block, 4 * columns), bf16),
         scratch_shapes=[
             pltpu.VMEM((half, width, wide), bf16),
-            pltpu.VMEM((rows, width), bf16),
+            pltpu.VMEM((2, rows, width), bf16),
+            pltpu.VMEM((2, rows, width), bf16),
             pltpu.VMEM((count, 4 * block, wide), f32),
             pltpu.VMEM((count, 4 * block, wide), bf16),
             pltpu.VMEM((count, 4 * block, wide), bf16),
@@ -527,28 +637,50 @@
         conv_bias_bc[None], conv_bias_bc[None], halo, halo, halo,
     )
 
-    gathered = lax.all_gather(sent, "seq")
-
-    y_local = pl.pallas_call(
-        local_kernel,
-        grid=(spans,),
-        in_specs=[
-            span_x,
-            span_bc,
-            span_bc,
-            span_dt,
-            const((heads, 1), 0, 0),
-            const((1, heads), 0, 0),
-            pl.BlockSpec((1, STATE, width), lambda i: (i, 0, 0)),
-        ],
-        out_specs=span_x,
-        out_shape=jax.ShapeDtypeStruct((rows, width), f32),
-        compiler_params=params(),
-        cost_estimate=pl.CostEstimate(
-            flops=4 * rows * width * STATE, bytes_accessed=rows * width * 8, transcendentals=0
-        ),
-        name="local_outputs",
-    )(conv_x, conv_b, conv_c, dt_input, rate, skip_weight[None], enter)
+    chained = seq_count == 4 and width % (PARTS * 128) == 0
+    local_specs = [
+        span_x,
+        span_bc,
+        span_bc,
+        span_dt,
+        const((heads, 1), 0, 0),
+        const((1, heads), 0, 0),
+        pl.BlockSpec((1, STATE, width), lambda i: (i, 0, 0)),
+    ]
+    local_args = (conv_x, conv_b, conv_c, dt_input, rate, skip_weight[None], enter)
+    y_shape = jax.ShapeDtypeStruct((rows, width), f32)
+    if chained:
+        slots = (PARTS, STATE + EXTRA, width // PARTS)
+        y_local, prior = pl.pallas_call(
+            chain_kernel,
+            grid=(spans,),
+            in_specs=local_specs
+            + [const((STATE, width), 0, 0), const((STATE + EXTRA, width), 0, 0)],
+            out_specs=[span_x, const((STATE + EXTRA, width), 0, 0)],
+            out_shape=[y_shape, jax.ShapeDtypeStruct((STATE + EXTRA, width), bf16)],
+            scratch_shapes=[
+                pltpu.VMEM(slots, bf16),
+                pltpu.VMEM(slots, bf16),
+                pltpu.SemaphoreType.DMA((PARTS,)),
+                pltpu.SemaphoreType.DMA((PARTS,)),
+            ],
+            compiler_params=pltpu.CompilerParams(
+                vmem_limit_bytes=VMEM_LIMIT, collective_id=1, has_side_effects=True
+            ),
+            name="local_outputs_and_chain",
+        )(*local_args, local, sent)
+        gathered = prior[None]
+    else:
+        gathered = lax.all_gather(sent, "seq")
+        y_local = pl.pallas_call(
+            local_kernel,
+            grid=(spans,),
+            in_specs=local_specs,
+            out_specs=span_x,
+            out_shape=y_shape,
+            compiler_params=params(),
+            name="local_outputs",
+        )(*local_args)
 
     bits = head_count.bit_length() - 1
     distance = jnp.arange(head_count, dtype=jnp.int32) ^ head_index
@@ -558,7 +690,9 @@
     meta = jnp.concatenate([seq_index[None].astype(jnp.int32), slot.astype(jnp.int32) * block])
 
     normed, boundary = pl.pallas_call(
-        functools.partial(output_kernel, block=block, whole_group=whole_group),
+        functools.partial(
+            output_kernel, block=block, whole_group=whole_group, chained=chained
+        ),
         grid_spec=pltpu.PrefetchScalarGridSpec(
             num_scalar_prefetch=1,
             grid=(spans,),
@@ -569,7 +703,8 @@
                 span_dt,
                 const((heads, 1), 0, 0),
                 const((1, width), 0, 0),
-                const((seq_count, STATE + EXTRA, width), 0, 0, 0),
+                const((gathered.shape[0], STATE + EXTRA, width), 0, 0, 0),
+                const((EXTRA, width), STATE // EXTRA, 0),
                 const((width, STATE), 0, 0),
                 const((STATE, width), 0, 0),
             ],
@@ -589,7 +724,7 @@
         name="gated_outputs",
     )(
         meta,
-        y_local, conv_c, gate_input, dt_input, rate, norm_gain[None], gathered,
+        y_local, conv_c, gate_input, dt_input, rate, norm_gain[None], gathered, sent,
         init_state.reshape(width, STATE), local,
     )
     boundary = boundary.reshape(1, heads, HEADDIM, STATE)

time: 215 us -> 190 us (0.88)
  waiting for transfers between devices: 34 us -> 7.62 us
  Pallas kernels: 148 us -> 165 us
  between operations: 14.1 us -> 0.73 us
  local copies, waits for them, and re-layouts: 14.9 us -> 11.9 us
    all_gather x1 -> x0, waiting for transfers between devices: 26.3 us -> none  [body(): gathered = lax.all_gather(sent, 'seq')]
    pallas_call x1, Pallas kernels: 111 us -> 127 us  [project(): pl.pallas_call(project_kernel, in_specs=[pl.BlockSpec(memory_space=pltpu....]
    pallas_call x1, Pallas kernels: 10.4 us -> 13.8 us  [body(): pl.pallas_call(chain_kernel, grid=(spans,), in_specs=local_specs + [const...]
    unnamed x27 -> x21, local copies, waits for them, and re-layouts: 11.8 us -> 8.81 us
  transfers between devices with their start and end apart: 3 -> 2, of which waited for: 2 -> 1; matrix products, arithmetic and copies ran while one was open for 2% -> 2% of each run, Pallas kernels for 17% -> 20%
where the time goes in v3:
time: 190 us; the launch traced here: 189 us
  Pallas kernels  165 us (87%)
  local copies, waits for them, and re-layouts  11.9 us (6%)
  waiting for transfers between devices  7.62 us (4%)
  starting transfers between devices  2.48 us (1%)
    pallas_call x1, Pallas kernels, project(): pl.pallas_call(project_kernel, in_specs=[pl.BlockSpec(memory_space=pltpu....  127 us
    pallas_call x1, Pallas kernels, body(): pl.pallas_call(chain_kernel, grid=(spans,), in_specs=local_specs + [const...  13.8 us
    pallas_call x1, Pallas kernels, body(): pl.pallas_call(functools.partial(output_kernel, block=block, whole_group=...  12.8 us
    pallas_call x1, Pallas kernels, body(): pl.pallas_call(state_kernel, grid_spec=pltpu.PrefetchScalarGridSpec(num_s...  12 us
    unnamed x21, local copies, waits for them, and re-layouts  8.81 us
    ppermute x1, waiting for transfers between devices, body(): lax.ppermute(last_rows, 'seq', [(i, i + 1) for i in range(seq_count - 1)])  7.61 us
  transfers between devices with their start and end apart: 2, of which 1 were waited for; matrix products, arithmetic and copies ran while one was open for 2% of the time, Pallas kernels for 20%

profile of v3, /device:TPU:0, one launch (start us, length us, event | category | flops | bytes accessed | tf_op | source)
XLA Modules:
  0.0 188.9 jit_solution(6837832069703849838)
XLA Ops:
  0.6 0.5 collective-permute-start.1
  1.1 0.9 slice.7
  2.0 0.8 slice.6
  2.8 2.0 %collective-permute-start = (bf16[3,2560]{1,0:T(4,128)(2,1)S(1)}, bf16[3,2560]{1,0:T(4,128)(2,1)S(1)}, u32[]{:S(2)}, u32[]{:S(2)}) collective-permute-start(bf16[3,2560]{1,0:T(4,128)(2,1)S(1)} %pad_maximum_fusion), channel_id=1, source_target_pairs={{0,8},{8,16},{16,24},{1,9},{9,17},{17,25},{2,10},{10,18},{18,26},{... | collective-permute-start | bytes 46088 | tf_op jit(solution)/shard_map/ppermute | solution.py:573
  4.8 0.7 constant_dynamic-slice_fusion.3
  5.5 0.1 pad_add_fusion.meta
  5.6 0.7 copy.17.rate
  6.3 7.6 %collective-permute-done = bf16[3,2560]{1,0:T(4,128)(2,1)S(1)} collective-permute-done((bf16[3,2560]{1,0:T(4,128)(2,1)S(1)}, bf16[3,2560]{1,0:T(4,128)(2,1)S(1)}, u32[]{:S(2)}, u32[]{:S(2)}) %collective-permute-start) | collective-permute-done | bytes 15392 | tf_op jit(solution)/shard_map/ppermute | solution.py:573
  14.0 0.7 maximum_select_fusion
  14.7 0.0 copy-start.2
  14.7 0.8 copy-done.2
  15.6 0.0 copy-start.4
  15.6 0.8 copy-done.4
  16.4 0.0 copy-start.5
  16.4 0.7 copy-done.5
  17.1 0.0 copy-start.6
  17.1 0.8 copy-done.6
  17.9 0.0 copy-start.7
  17.9 0.7 copy-done.7
  18.6 0.0 copy-start.3
  18.6 0.0 copy-start.9
  18.6 12.0 %conv_and_states.1 = (bf16[512,2048]{1,0:T(8,128)(2,1)S(1)}, bf16[512,256]{1,0:T(8,128)(2,1)S(1)}, bf16[512,256]{1,0:T(8,128)(2,1)S(1)}, bf16[4,256,2048]{2,1,0:...) custom-call(s32[1]{0:T(128)} %bitcast.1.g_ref, bf16[512,2048]{1,0:T(8,128)(2,1)} %inner.1, ...), custom_call_target="tpu_custom_call" | custom-call | tf_op jit(solution)/shard_map/conv_and_states/pallas_call | solution.py:586
  30.6 0.0 copy-start
  30.6 1.3 copy-done
  31.9 0.0 copy-done.3
  31.9 0.0 copy-done.9
  32.0 0.0 copy-start.8
  32.0 13.8 %local_outputs_and_chain.1 = (f32[512,2048]{1,0:T(8,128)}, bf16[272,2048]{1,0:T(8,128)(2,1)S(1)}) custom-call(bf16[512,2048]{1,0:T(8,128)(2,1)S(1)} %get-tuple-element.12.x, bf16[512,256]{1,0:T(8,128)(2,1)S(1)} %get-tuple-element.13.b, bf16[512,256]{1,0:T(8,128)(2,1)S(1)} %get-tuple-element.14.c, f32[32,512]{1,0:T(8,128)S(1)} %copy-done.3, ...), custom_call_target="tpu_custom_call" | custom-call | tf_op jit(solution)/shard_map/local_outputs_and_chain/pallas_call | solution.py:654
  45.8 0.0 copy-done.8
  45.8 12.8 %gated_outputs.1 = (bf16[512,2048]{1,0:T(8,128)(2,1)S(1)}, f32[2048,256]{1,0:T(8,128)}) custom-call(s32[9]{0:T(128)S(1)} %pad_add_fusion.meta, f32[512,2048]{1,0:T(8,128)} %get-tuple-element.18.y, bf16[512,256]{1,0:T(8,128)(2,1)S(1)} %get-tuple-element.14.c, bf16[512,2048]{1,0:T(8,128)(2,1)} %gate.1, f32[32,512]{1,0:T(8,128)S(1)} %copy-done.3, ...), custom_call_target="tpu_custom_call" | custom-call | tf_op jit(solution)/shard_map/gated_outputs/pallas_call | solution.py:692
  58.6 0.0 copy-start.1
  58.6 1.4 copy-done.1
  60.0 0.0 collective-permute-done.1.w_other
  60.0 126.7 %project_and_sum.1 = bf16[64,8192]{1,0:T(8,128)(2,1)} custom-call(bf16[512,2048]{1,0:T(8,128)(2,1)} %copy-done.1, bf16[2048,2048]{1,0:T(8,128)(2,1)} %w_own.1, bf16[2048,2048]{1,0:T(8,128)(2,1)} %collective-permute-done.1.w_other), custom_call_target="tpu_custom_call" | custom-call | tf_op jit(solution)/shard_map/project_and_sum/pallas_call | solution.py:492
  186.6 2.3 %copy.21 = bf16[64,8192]{1,0:T(8,128)(2,1)} copy(bf16[64,8192]{1,0:T(8,128)(2,1)} %project_and_sum.1) | data formatting | bytes 2097152
  (4 shorter events, 0.1 us)
Async XLA Ops:
  0.6 59.4 %collective-permute-start.1 = (bf16[2048,2048]{1,0:T(8,128)(2,1)}, bf16[2048,2048]{1,0:T(8,128)(2,1)}, u32[]{:S(2)}, u32[]{:S(2)}) collective-permute-start(bf16[2048,2048]{1,0:T(8,128)(2,1)} %w_own.1), channel_id=1, source_target_pairs={{0,8},{8,0},{16,24},{24,16},{1,9},{9,1},{17,25},{25,17},{2,10},{10... | collective-permute-start | bytes 25165832 | tf_op jit(solution)/shard_map/ppermute | solution.py:562
  2.8 11.1 %collective-permute-start = (bf16[3,2560]{1,0:T(4,128)(2,1)S(1)}, bf16[3,2560]{1,0:T(4,128)(2,1)S(1)}, u32[]{:S(2)}, u32[]{:S(2)}) collective-permute-start(bf16[3,2560]{1,0:T(4,128)(2,1)S(1)} %pad_maximum_fusion), channel_id=1, source_target_pairs={{0,8},{8,16},{16,24},{1,9},{9,17},{17,25},{2,10},{10,18},{18,26},{... | collective-permute-start | bytes 46088 | tf_op jit(solution)/shard_map/ppermute | solution.py:573
  14.7 0.8 copy-start.2
  15.6 0.8 copy-start.4
  16.4 0.7 copy-start.5
  17.1 0.8 copy-start.6
  17.9 0.7 copy-start.7
  18.6 13.4 %copy-start.3 = (f32[32,512]{1,0:T(8,128)S(1)}, f32[32,512]{1,0:T(8,128)}, u32[]{:S(2)}) copy-start(f32[32,512]{1,0:T(8,128)} %dt.5) | copy-start | bytes 196612
  18.6 13.4 %copy-start.9 = (f32[32]{0:T(128)S(1)}, f32[32]{0:T(128)}, u32[]{:S(2)}) copy-start(f32[32]{0:T(128)} %param.20) | copy-start | bytes 388
  30.6 1.3 copy-start
  32.0 13.8 %copy-start.8 = (f32[2048]{0:T(1024)S(1)}, f32[2048]{0:T(1024)}, u32[]{:S(2)}) copy-start(f32[2048]{0:T(1024)} %param.28) | copy-start | bytes 24580
  58.6 1.4 copy-start.1
